TPU v7x, 32 devices: a whole 2x2x4 slice. The times are simulated.
32 devices in a mesh: parts: 2 (over y), seq: 4 (over z), chan: 4 (over x, core).
Axes of the slice: x: 2, y: 2, z: 4, core: 2. Of those that a mesh axis runs over, the one named last changes fastest.
Arguments:
- x_tokens: bfloat16 [64, 8192], P(('parts', 'seq'), 'chan'), parts along dimension 0, may hold values from -6 to 6
- norm_gain: float32 [8192], P('chan'), may hold values from 0.5 to 1.5
- w_in: bfloat16 [3, 8192, 8192], P(None, 'seq', 'chan'), may hold values from -0.0625 to 0.0625
- short_filter: float32 [3, 3, 8192], P(None, None, 'seq'), may hold values from -3 to 3
- se_filter: float32 [7, 512], P(None, 'seq'), may hold values from -2 to 2
- w_out: bfloat16 [8192, 8192], P('seq'), may hold values from -0.0625 to 0.0625
Outputs:
- mixed_out: bfloat16 [64, 8192], P(('parts', 'chan'), 'seq'), parts along dimension 0
There are 2 independent parts, one for each index of `parts`. A program takes and returns all parts, laid end to end along the dimension named above; an argument that names none is the same for every part. Nothing has to cross between parts.
All inputs are finite; a program needn't handle non-finite values.
Results may differ from a plain program's by a relative error of at most 0.0086.
Values may be sent and summed in bfloat16 or wider, within the bound.
No kernel may reach another device: no remote copies, remote signals or barrier semaphores. Data moves between devices by JAX's collectives and lax.ppermute only.
A program may use at most 128 MiB of HBM per device.

v0:
```python
import jax
import jax.numpy as jnp
from jax import lax
from jax.sharding import PartitionSpec as P

D = 8192
GROUP = 16


epsilon = 1e-06


def from_behind(value, axis, steps):
    count = lax.axis_size(axis)
    leading, last = (max(0, -steps), min(count, count - steps))
    return lax.ppermute(value, axis, [(source, source + steps) for source in range(leading, last)])


def mixer(extended, short_taps, long_taps):
    wide = extended.astype(jnp.float32)
    row_count = wide.shape[0]
    featured = sum(
        (short_taps[offset] * wide[2 - offset : row_count - offset] for offset in range(3))
    )
    queries = featured[:, 0]
    product = featured[:, 1] * featured[:, 2]
    length = product.shape[0]
    filtered = sum(
        (long_taps[offset] * product[6 - offset : length - offset] for offset in range(7))
    )
    return (queries[6:] * filtered).astype(jnp.bfloat16)


def contract_last(left, right):
    return lax.dot_general(
        left, right, (((1,), (1,)), ((), ())), preferred_element_type=jnp.float32
    )


def shards(x_tokens, norm_gain, w_in, short_filter, se_filter, w_out):
    wide = x_tokens.astype(jnp.float32)
    local_squares = jnp.sum(wide * wide, axis=1, keepdims=True)
    total_squares = lax.psum(local_squares, "chan")
    factor = lax.rsqrt(total_squares / D + epsilon)
    normed = (wide * factor * norm_gain).astype(jnp.bfloat16)
    columns = w_in.shape[1]
    flat_in = w_in.reshape(3 * columns, w_in.shape[2])
    piece = lax.all_gather(normed, "seq", axis=0, tiled=True)
    partial_terms = contract_last(piece, flat_in).reshape(piece.shape[0], 3, columns)
    long_full = jnp.repeat(se_filter, GROUP, axis=1)
    mine = lax.psum_scatter(partial_terms, "chan", scatter_dimension=0, tiled=True).astype(
        jnp.bfloat16
    )
    previous = from_behind(mine[-8:], "chan", 1)
    extended = jnp.concatenate([previous, mine], axis=0)
    gated = mixer(extended, short_filter, long_full)
    result = contract_last(lax.all_gather(gated, "seq", axis=1, tiled=True), w_out)
    return result.astype(jnp.bfloat16)


def solution(mesh):
    placed = (
        P(("parts", "seq"), "chan"),
        P("chan"),
        P(None, "seq", "chan"),
        P(None, None, "seq"),
        P(None, "seq"),
        P("seq", None),
    )
    return jax.shard_map(
        shards, mesh=mesh, in_specs=placed, out_specs=P(("parts", "chan"), "seq"), check_vma=False
    )
```

profile of v0, /device:TPU:0, one launch (start us, length us, event | category | flops | bytes accessed | tf_op | source)
XLA Modules:
  0.0 107.5 jit_solution(7954886832939469192)
XLA Ops:
  6.5 0.0 reduce-scatter.2.cloned.1.call-start
  6.5 0.9 fusion.4
  7.4 8.4 %psum.7 = f32[8,1]{0,1:T(1,128)S(1)} all-reduce(f32[8,1]{0,1:T(1,128)S(1)} %bitcast.89), channel_id=1, replica_groups=mesh['parts'=2,'seq'=4,'chan'=4] {'chan'}, use_global_device_ids=true, to_apply=%region_1.0 | all-reduce | flops 8 | bytes 64 | tf_op jit(solution)/shard_map/psum | solution.py:43
  15.8 0.8 fusion.6
  16.6 13.6 %all_gather.6 = bf16[32,2048]{1,0:T(8,128)(2,1)S(1)} all-gather(bf16[8,2048]{1,0:T(8,128)(2,1)S(1)} %fusion.6), channel_id=1, replica_groups=mesh['parts'=2,'seq'=4,'chan'=4] {'seq'}, dimensions={0}, use_global_device_ids=true | all-gather | bytes 163840 | tf_op jit(solution)/shard_map/all_gather | solution.py:48
  30.2 13.0 %fusion.2 = f32[32,3,2048]{2,0,1:T(8,128)} fusion(bf16[3,2048,2048]{2,1,0:T(8,128)(2,1)} %param.8, bf16[32,2048]{1,0:T(8,128)(2,1)S(1)} %all_gather.6), kind=kOutput, calls=%fused_computation.8 | convolution fusion | flops 805306368 | bytes 26083328 | tf_op jit(solution)/shard_map/dot_general | solution.py:35
  43.3 0.0 reduce-scatter.2.cloned.1.call-update
  43.3 0.8 slice_bitcast_fusion.10
  44.1 22.8 %reduce-scatter.2.cloned.1.call-done = f32[8,3,2048]{2,0,1:T(8,128)} async-done(((f32[32,3,2048]{2,0,1:T(8,128)}), f32[8,3,2048]{2,0,1:T(8,128)}) %reduce-scatter.2.cloned.1.call-update) | async-done | bytes 196624 | tf_op jit(solution)/shard_map/reduce_scatter | solution.py:51
  66.9 0.9 convert_element_type.20
  67.9 1.6 %collective-permute-start = (bf16[8,3,2048]{2,0,1:T(8,128)(2,1)S(1)}, bf16[8,3,2048]{2,0,1:T(8,128)(2,1)S(1)}, u32[]{:S(2)}, u32[]{:S(2)}) collective-permute-start(bf16[8,3,2048]{2,0,1:T(8,128)(2,1)S(1)} %convert_element_type.20), channel_id=1, source_target_pairs={{0,1},{1,2},{2,3},{4,5},{5,6},{6,7},{8,9},{9,10},{10,11},{12,13},{... | collective-permute-start | bytes 294920 | tf_op jit(solution)/shard_map/ppermute | solution.py:16
  69.4 0.9 slice_bitcast_fusion.17
  70.4 0.1 broadcast_in_dim.34
  70.5 0.1 broadcast_in_dim.35
  70.6 0.1 broadcast_in_dim.36
  70.6 0.1 broadcast_in_dim.37
  70.7 0.1 broadcast_in_dim.38
  70.8 0.1 broadcast_in_dim.39
  70.9 0.1 broadcast_in_dim.40
  71.0 0.1 broadcast_in_dim.41
  71.1 0.1 broadcast_in_dim.42
  71.1 0.1 broadcast_in_dim.43
  71.2 0.1 broadcast_in_dim.44
  71.3 0.1 broadcast_in_dim.45
  71.4 0.1 broadcast_in_dim.46
  71.5 0.1 broadcast_in_dim.47
  71.6 0.0 collective-permute-done
  71.6 0.1 fusion
  71.8 0.1 fusion.10
  71.8 13.7 %all_gather.7 = bf16[8,8192]{1,0:T(8,128)(2,1)S(1)} all-gather(bf16[8,2048]{1,0:T(8,128)(2,1)S(1)} %fusion.10), channel_id=1, replica_groups=mesh['parts'=2,'seq'=4,'chan'=4] {'seq'}, dimensions={1}, use_global_device_ids=true | all-gather | bytes 163840 | tf_op jit(solution)/shard_map/all_gather | solution.py:57
  85.5 15.1 %convolution_convert_fusion = bf16[8,2048]{1,0:T(8,128)(2,1)} fusion(bf16[8,8192]{1,0:T(8,128)(2,1)S(1)} %all_gather.7, bf16[2048,8192]{1,0:T(8,128)(2,1)} %param.11), kind=kOutput, calls=%fused_computation | convolution fusion | flops 268451840 | bytes 33718272 | tf_op jit(solution)/shard_map/dot_general | solution.py:35
  (3 shorter events, 0.1 us)
Async XLA Ops:
  6.5 60.4 %reduce-scatter.2.cloned.1.call-start = ((), (), s32[]{:S(2)}) async-start(), calls=%async_computation.1 | async-start | bytes 983040 | tf_op jit(solution)/shard_map/reduce_scatter | solution.py:51
  67.9 3.7 %collective-permute-start = (bf16[8,3,2048]{2,0,1:T(8,128)(2,1)S(1)}, bf16[8,3,2048]{2,0,1:T(8,128)(2,1)S(1)}, u32[]{:S(2)}, u32[]{:S(2)}) collective-permute-start(bf16[8,3,2048]{2,0,1:T(8,128)(2,1)S(1)} %convert_element_type.20), channel_id=1, source_target_pairs={{0,1},{1,2},{2,3},{4,5},{5,6},{6,7},{8,9},{9,10},{10,11},{12,13},{... | collective-permute-start | bytes 294920 | tf_op jit(solution)/shard_map/ppermute | solution.py:16
Sparse Core Ops, SparseCore 0:
  43.4 23.4 reduce-scatter.1
where the time goes:
time: 108 us; the launch traced here: 107 us
  blocking collectives  35.7 us (33%)
  matrix products  28.1 us (26%)
  waiting for transfers between devices  22.8 us (21%)
  between operations  13.4 us (12%)
  local copies, waits for them, and re-layouts  2.93 us (3%)
  other arithmetic  2.92 us (3%)
  starting transfers between devices  1.56 us (1%)
    dot_general x2, matrix products, contract_last(): lax.dot_general(left, right, (((1,), (1,)), ((), ())), preferred_element_...  28.1 us
    reduce_scatter x1, waiting for transfers between devices, shards(): lax.psum_scatter(partial_terms, 'chan', scatter_dimension=0, tiled=True)  22.8 us
    all_gather x1, blocking collectives, shards(): lax.all_gather(gated, 'seq', axis=1, tiled=True)  13.7 us
    all_gather x1, blocking collectives, shards(): piece = lax.all_gather(normed, 'seq', axis=0, tiled=True)  13.6 us
    psum x1, blocking collectives, shards(): total_squares = lax.psum(local_squares, 'chan')  8.36 us
  transfers between devices with their start and end apart: 2, of which 1 were waited for; matrix products, arithmetic and copies ran while one was open for 3% of the time, Pallas kernels for 0%

commit v1 on v0

v1 whole, which is shorter than its diff:
```python
import functools

import jax
import jax.numpy as jnp
from jax import lax
from jax.experimental import pallas as pl
from jax.experimental.pallas import tpu as pltpu
from jax.sharding import PartitionSpec as P

GROUP = 16
epsilon = 1e-06
LANES = 128
PACK = 4
VMEM = pl.BlockSpec(memory_space=pltpu.VMEM)
ANY = pl.BlockSpec(memory_space=pl.ANY)
F32, BF16 = jnp.float32, jnp.bfloat16


def contract_last(left, right):
    return lax.dot_general(left, right, (((1,), (1,)), ((), ())), preferred_element_type=F32)


def spread(rows):
    blank = jnp.zeros_like(rows)
    return [jnp.concatenate([rows if i == q else blank for i in range(PACK)], axis=0) for q in range(PACK)]


def call(body, outs, ins, scratch=(), limit=2, cost=None):
    return pl.pallas_call(
        body,
        out_shape=outs,
        in_specs=ins,
        out_specs=jax.tree.map(lambda _: VMEM, outs),
        scratch_shapes=list(scratch),
        compiler_params=pltpu.CompilerParams(vmem_limit_bytes=limit << 20),
        cost_estimate=cost,
    )


def struct(shape, dtype):
    return jax.ShapeDtypeStruct(shape, dtype)


def open_body(x_ref, o_ref):
    o_ref[...] = x_ref[...]


def taps_body(se, out):
    groups, quarter = se.shape[1], out.shape[1]
    first = lax.axis_index("chan") * (quarter // GROUP)
    row = lax.broadcasted_iota(jnp.int32, (groups, quarter), 0)
    column = lax.broadcasted_iota(jnp.int32, (groups, quarter), 1)
    chosen = jnp.where(row == first + column // GROUP, 1.0, 0.0).astype(BF16)
    rest, total = se[...], 0.0
    for _ in range(3):
        part = rest.astype(BF16)
        total = total + jnp.dot(part, chosen, preferred_element_type=F32)
        rest = rest - part.astype(F32)
    out[...] = total


def high_low(squares):
    high = squares.astype(BF16).astype(F32)
    low = (squares - high).astype(BF16).astype(F32)
    lane = lax.broadcasted_iota(jnp.int32, (8, LANES), 1)
    count = squares.shape[0] // 8
    return jnp.concatenate(
        [jnp.where(lane < LANES // 2, high[8 * i : 8 * i + 8], low[8 * i : 8 * i + 8]) for i in range(count)], axis=1
    )


def from_high_low(packed, count):
    return jnp.concatenate(
        [packed[:, i * LANES : i * LANES + 1] + packed[:, i * LANES + LANES // 2 : i * LANES + LANES // 2 + 1] for i in range(count)],
        axis=0,
    )


def project_body(seq, quarter, *refs):
    pieces, (gain, w_in), (send, keep), (wide,) = refs[:seq], refs[seq : seq + 2], refs[seq + 2 : seq + 4], refs[seq + 4 :]
    s, c = lax.axis_index("seq"), lax.axis_index("chan")
    rows = pieces[0].shape[0]
    for hop in range(seq):
        place = pl.multiple_of(jnp.bitwise_xor(s, hop) * rows, rows)
        wide[pl.ds(place, rows), :] = pieces[hop][...].astype(F32)
    tokens = wide[...]
    squares = jnp.sum(tokens * tokens, axis=1, keepdims=True)
    packs = spread((tokens * gain[...]).astype(BF16))
    count = tokens.shape[0]
    half = quarter // 2
    for other in (1, 0):
        for comp in range(3):
            total = None
            for chip in range(2):
                owner = jnp.bitwise_xor(c, 2 * chip + other)
                for h in range(2):
                    start = pl.multiple_of(owner * quarter + h * half, half)
                    term = contract_last(w_in[comp, pl.ds(start, half), :], packs[2 * chip + h])
                    total = term if total is None else total + term
            flipped = total.T
            for chip in range(2):
                value = flipped[2 * chip * count : 2 * (chip + 1) * count]
                if other:
                    send[chip, : 2 * count, comp * half : (comp + 1) * half] = value.astype(BF16)
                else:
                    keep[chip, : 2 * count, comp * half : (comp + 1) * half] = value
    packed = high_low(squares)
    width = packed.shape[1]
    for chip in range(2):
        keep[chip, 2 * count :, :width] = packed
        send[chip, 2 * count :, :width] = packed.astype(BF16)
        keep[chip, 2 * count :, width:] = jnp.zeros((8, 3 * half - width), F32)
        send[chip, 2 * count :, width:] = jnp.zeros((8, 3 * half - width), BF16)


def relay_body(rows, keep, got, out):
    value = keep[1] + got[1].astype(F32)
    out[:rows, :] = value[:rows].astype(BF16)
    count = rows // 16
    width = count * LANES
    packed = high_low(from_high_low(value[rows:], count))
    out[rows:, :width] = packed.astype(BF16)
    out[rows:, width:] = jnp.zeros((8, value.shape[1] - width), BF16)


def later(value, lag):
    if lag == 0:
        return value
    return jnp.concatenate([jnp.zeros((lag, value.shape[1]), value.dtype), value[: value.shape[0] - lag]], axis=0)


def mix_body(features, keep, near, far, short, long_ref, out):
    c = lax.axis_index("chan")
    value = keep[0] + near[0].astype(F32) + far[...].astype(F32)
    rows = value.shape[0] - 8
    count = rows // 2
    half = value.shape[1] // 3
    squares = from_high_low(value[rows:], count // 8)
    factor = lax.rsqrt(squares / features + epsilon)
    for h in range(2):
        scaled = value[h * count : (h + 1) * count] * factor
        start = pl.multiple_of(c * (2 * half) + h * half, LANES)
        featured = []
        for comp in range(3):
            part = scaled[:, comp * half : (comp + 1) * half]
            taps = [short[lag, comp : comp + 1, pl.ds(start, half)] for lag in range(3)]
            featured.append(sum(taps[lag] * later(part, lag) for lag in range(3)))
        product = featured[1] * featured[2]
        filtered = sum(
            long_ref[lag : lag + 1, h * half : (h + 1) * half] * later(product, lag) for lag in range(long_ref.shape[0])
        )
        out[:, h * half : (h + 1) * half] = (featured[0] * filtered).astype(BF16)


def output_body(seq, quarter, *refs):
    pieces, w_out, (send, keep), (wide,) = refs[:seq], refs[seq], refs[seq + 1 : seq + 3], refs[seq + 3 :]
    s, c = lax.axis_index("seq"), lax.axis_index("chan")
    outputs = w_out.shape[0]
    block = w_out.shape[1] // seq
    part = outputs // PACK
    count = pieces[0].shape[0]
    total = None
    for hop in range(seq):
        source = jnp.bitwise_xor(s, hop)
        start = pl.multiple_of(source * block + c * quarter, LANES)
        packs = spread(pieces[hop][...])
        for q in range(PACK):
            term = contract_last(w_out[q * part : (q + 1) * part, pl.ds(start, quarter)], packs[q])
            total = term if total is None else total + term
    flipped = total.T
    for q in range(PACK):
        wide[:, q * part : (q + 1) * part] = flipped[q * count : (q + 1) * count]
    rows = send.shape[1]
    for chip in range(2):
        for other in range(2):
            owner = jnp.bitwise_xor(c, 2 * chip + other)
            value = wide[pl.ds(pl.multiple_of(owner * rows, rows), rows), :]
            if other:
                send[chip] = value.astype(BF16)
            else:
                keep[chip] = value


def pass_body(keep, got, out):
    out[...] = (keep[1] + got[1].astype(F32)).astype(BF16)


def close_body(keep, near, far, out):
    out[...] = (keep[0] + near[0].astype(F32) + far[...].astype(F32)).astype(BF16)


def swap(value, axis, bit):
    return lax.ppermute(value, axis, [(i, i ^ bit) for i in range(lax.axis_size(axis))])


def gathered(value, axis):
    return [value] + [swap(value, axis, bit) for bit in range(1, lax.axis_size(axis))]


def short_shards(x_tokens, norm_gain, w_in, short_filter, se_filter, w_out):
    seq, chan = lax.axis_size("seq"), lax.axis_size("chan")
    rows, columns = x_tokens.shape
    tokens, block = rows * seq, w_in.shape[1]
    quarter = block // chan
    wide_rows, wide_columns = 2 * tokens + 8, 3 * quarter // 2

    ahead = lambda weights, times: pl.CostEstimate(
        flops=times * 100 * weights.size * tokens, transcendentals=0, bytes_accessed=times * 8 * weights.size
    )
    x_tokens = call(open_body, struct(x_tokens.shape, BF16), [VMEM], limit=1, cost=ahead(w_in, 2))(x_tokens)
    pieces = gathered(x_tokens, "seq")
    held_in = pltpu.with_memory_space_constraint(w_in, pltpu.VMEM)
    long_taps = call(taps_body, struct((se_filter.shape[0], quarter), F32), [VMEM])(se_filter)
    send, keep = call(
        functools.partial(project_body, seq, quarter),
        (
            struct((2, wide_rows, wide_columns), BF16),
            struct((2, wide_rows, wide_columns), F32),
        ),
        [VMEM] * (seq + 2),
        scratch=[pltpu.VMEM((tokens, columns), F32)],
        limit=10,
    )(*pieces, norm_gain.reshape(1, columns), held_in)
    near = swap(send, "chan", 1)
    relay = call(
        functools.partial(relay_body, 2 * tokens), struct((wide_rows, wide_columns), BF16), [VMEM] * 2, cost=ahead(w_out, 4)
    )(keep, near)
    far = swap(relay, "chan", 2)
    gated = call(
        functools.partial(mix_body, columns * chan), struct((tokens, quarter), BF16), [VMEM] * 5
    )(keep, near, far, short_filter, long_taps)
    pieces = gathered(gated, "seq")
    outputs = w_out.shape[0]
    send, keep = call(
        functools.partial(output_body, seq, quarter),
        (struct((2, tokens // chan, outputs), BF16), struct((2, tokens // chan, outputs), F32)),
        [VMEM] * (seq + 1),
        scratch=[pltpu.VMEM((tokens, outputs), F32)],
        limit=6,
    )(*pieces, pltpu.with_memory_space_constraint(w_out, pltpu.VMEM))
    near = swap(send, "chan", 1)
    relay = call(pass_body, struct((tokens // chan, outputs), BF16), [VMEM] * 2)(keep, near)
    far = swap(relay, "chan", 2)
    return call(close_body, struct((tokens // chan, outputs), BF16), [VMEM] * 3)(keep, near, far)


def from_behind(value, axis, steps):
    count = lax.axis_size(axis)
    leading, last = max(0, -steps), min(count, count - steps)
    return lax.ppermute(value, axis, [(source, source + steps) for source in range(leading, last)])


def mixer(extended, short_taps, long_taps):
    wide = extended.astype(F32)
    row_count = wide.shape[0]
    featured = sum(short_taps[offset] * wide[2 - offset : row_count - offset] for offset in range(3))
    product = featured[:, 1] * featured[:, 2]
    length = product.shape[0]
    filtered = sum(long_taps[offset] * product[6 - offset : length - offset] for offset in range(7))
    return (featured[6:, 0] * filtered).astype(BF16)


def long_shards(x_tokens, norm_gain, w_in, short_filter, se_filter, w_out):
    features = x_tokens.shape[1] * lax.axis_size("chan")
    wide = x_tokens.astype(F32)
    squares = lax.psum(jnp.sum(wide * wide, axis=1, keepdims=True), "chan")
    normed = (wide * lax.rsqrt(squares / features + epsilon) * norm_gain).astype(BF16)
    columns = w_in.shape[1]
    flat_in = w_in.reshape(3 * columns, w_in.shape[2])
    piece = lax.all_gather(normed, "seq", axis=0, tiled=True)
    terms = contract_last(piece, flat_in).reshape(piece.shape[0], 3, columns)
    mine = lax.psum_scatter(terms, "chan", scatter_dimension=0, tiled=True).astype(BF16)
    extended = jnp.concatenate([from_behind(mine[-8:], "chan", 1), mine], axis=0)
    gated = mixer(extended, short_filter, jnp.repeat(se_filter, GROUP, axis=1))
    return contract_last(lax.all_gather(gated, "seq", axis=1, tiled=True), w_out).astype(BF16)


def shards(x_tokens, norm_gain, w_in, short_filter, se_filter, w_out):
    seq, chan = lax.axis_size("seq"), lax.axis_size("chan")
    rows, block = x_tokens.shape[0], w_in.shape[1]
    fits = (
        chan == 4
        and seq == 4
        and rows % 8 == 0
        and rows * seq <= 64
        and block % (2 * LANES * chan) == 0
        and w_out.shape[0] % (PACK * LANES) == 0
        and 2 * w_in.size <= 30 << 20
    )
    return (short_shards if fits else long_shards)(x_tokens, norm_gain, w_in, short_filter, se_filter, w_out)


def solution(mesh):
    placed = (
        P(("parts", "seq"), "chan"),
        P("chan"),
        P(None, "seq", "chan"),
        P(None, None, "seq"),
        P(None, "seq"),
        P("seq", None),
    )
    return jax.shard_map(shards, mesh=mesh, in_specs=placed, out_specs=P(("parts", "chan"), "seq"), check_vma=False)
```

time: 108 us -> 42 us (0.39)
  blocking collectives: 35.7 us -> 0 us
  matrix products: 28.1 us -> 0 us
  between operations: 13.4 us -> 0.07 us
  starting transfers between devices: 1.56 us -> 13.3 us
  Pallas kernels: 0 us -> 10.4 us
  waiting for transfers between devices: 22.8 us -> 17.1 us
  other arithmetic: 2.92 us -> 0 us
  local copies, waits for them, and re-layouts: 2.93 us -> 0.93 us
    dot_general x2 -> x0, matrix products: 28.1 us -> none  [contract_last(): lax.dot_general(left, right, (((1,), (1,)), ((), ())), preferred_element_...]
    all_gather x2 -> x0, blocking collectives: 27.3 us -> none  [the longest x1 13.7 us: shards(): lax.all_gather(gated, 'seq', axis=1, tiled=True)]
    reduce_scatter x1 -> x0, waiting for transfers between devices: 22.8 us -> none  [shards(): lax.psum_scatter(partial_terms, 'chan', scatter_dimension=0, tiled=True)]
    ppermute x1 -> x10, waiting for transfers between devices: 0.01 us -> 17.1 us  [swap(): lax.ppermute(value, axis, [(i, i ^ bit) for i in range(lax.axis_size(axis...]
    ppermute x1 -> x10, starting transfers between devices: 1.56 us -> 13.3 us  [swap(): lax.ppermute(value, axis, [(i, i ^ bit) for i in range(lax.axis_size(axis...]
    pallas_call x0 -> x8, Pallas kernels: none -> 10.4 us  [the longest x1 6.74 us: short_shards(): call(functools.partial(project_body, seq, quarter), (struct((2, wide_rows...]
    psum x1 -> x0, blocking collectives: 8.36 us -> none  [shards(): total_squares = lax.psum(local_squares, 'chan')]
    convert_element_type x4 -> x0, other arithmetic: 1.88 us -> none  [the longest x1 0.94 us: shards(): lax.psum_scatter(partial_terms, 'chan', scatter_dimension=0, tiled=True)]
  transfers between devices with their start and end apart: 2 -> 10, of which waited for: 1 -> 8; matrix products, arithmetic and copies ran while one was open for 3% -> 0% of each run, Pallas kernels for 0% -> 0%
where the time goes in v1:
time: 42 us; the launch traced here: 41.9 us
  waiting for transfers between devices  17.1 us (41%)
  starting transfers between devices  13.3 us (32%)
  Pallas kernels  10.4 us (25%)
  local copies, waits for them, and re-layouts  0.93 us (2%)
    ppermute x10, waiting for transfers between devices, swap(): lax.ppermute(value, axis, [(i, i ^ bit) for i in range(lax.axis_size(axis...  17.1 us
    ppermute x10, starting transfers between devices, swap(): lax.ppermute(value, axis, [(i, i ^ bit) for i in range(lax.axis_size(axis...  13.3 us
    pallas_call x1, Pallas kernels, short_shards(): call(functools.partial(project_body, seq, quarter), (struct((2, wide_rows...  6.74 us
    pallas_call x1, Pallas kernels, short_shards(): call(functools.partial(output_body, seq, quarter), (struct((2, tokens //...  2.46 us
    unnamed x12, local copies, waits for them, and re-layouts  0.93 us
  transfers between devices with their start and end apart: 10, of which 8 were waited for; matrix products, arithmetic and copies ran while one was open for 0% of the time, Pallas kernels for 0%

profile of v1, /device:TPU:0, one launch (start us, length us, event | category | flops | bytes accessed | tf_op | source)
XLA Modules:
  0.0 41.9 jit_solution(3160746428605716868)
XLA Ops:
  0.0 0.0 copy-start.3
  0.0 0.0 copy-start.1
  0.0 0.0 copy-start.5
  0.0 0.9 %copy-done.5 = bf16[8,2048]{1,0:T(8,128)(2,1)S(1)} copy-done((bf16[8,2048]{1,0:T(8,128)(2,1)S(1)}, bf16[8,2048]{1,0:T(8,128)(2,1)}, u32[]{:S(2)}) %copy-start.5) | copy-done | bytes 32792
  0.9 3.1 %collective-permute-start = (bf16[8,2048]{1,0:T(8,128)(2,1)S(1)}, bf16[8,2048]{1,0:T(8,128)(2,1)S(1)}, u32[]{:S(2)}, u32[]{:S(2)}) collective-permute-start(bf16[8,2048]{1,0:T(8,128)(2,1)S(1)} %shard_map.64.refs_0_), channel_id=1, source_target_pairs={{0,4},{4,0},{8,12},{12,8},{1,5},{5,1},{9,13},{13,9},{2,6},{6,2},{1... | collective-permute-start | bytes 98312 | tf_op jit(solution)/shard_map/ppermute | solution.py:193
  4.0 2.6 %collective-permute-start.1 = (bf16[8,2048]{1,0:T(8,128)(2,1)S(1)}, bf16[8,2048]{1,0:T(8,128)(2,1)S(1)}, u32[]{:S(2)}, u32[]{:S(2)}) collective-permute-start(bf16[8,2048]{1,0:T(8,128)(2,1)S(1)} %shard_map.64.refs_0_), channel_id=1, source_target_pairs={{0,8},{4,12},{8,0},{12,4},{1,9},{5,13},{9,1},{13,5},{2,10},{6,14},... | collective-permute-start | bytes 98312 | tf_op jit(solution)/shard_map/ppermute | solution.py:193
  6.6 0.0 collective-permute-start.2
  6.6 0.0 collective-permute-done.refs_1_
  6.6 2.8 %collective-permute-done.1.refs_2_ = bf16[8,2048]{1,0:T(8,128)(2,1)S(1)} collective-permute-done((bf16[8,2048]{1,0:T(8,128)(2,1)S(1)}, bf16[8,2048]{1,0:T(8,128)(2,1)S(1)}, u32[]{:S(2)}, u32[]{:S(2)}) %collective-permute-start.1) | collective-permute-done | bytes 32800 | tf_op jit(solution)/shard_map/ppermute | solution.py:193
  9.4 2.9 %collective-permute-done.2.refs_3_ = bf16[8,2048]{1,0:T(8,128)(2,1)S(1)} collective-permute-done((bf16[8,2048]{1,0:T(8,128)(2,1)S(1)}, bf16[8,2048]{1,0:T(8,128)(2,1)S(1)}, u32[]{:S(2)}, u32[]{:S(2)}) %collective-permute-start.2) | collective-permute-done | bytes 32800 | tf_op jit(solution)/shard_map/ppermute | solution.py:193
  12.3 0.0 copy-done.3
  12.3 0.0 copy-done.1
  12.3 6.7 %shard_map.65 = (bf16[2,72,768]{2,1,0:T(8,128)(2,1)S(1)}, f32[2,72,768]{2,1,0:T(8,128)S(1)}) custom-call(bf16[8,2048]{1,0:T(8,128)(2,1)S(1)} %shard_map.64.refs_0_, bf16[8,2048]{1,0:T(8,128)(2,1)S(1)} %collective-permute-done.refs_1_, bf16[8,2048]{1,0:T(8,128)(2,1)S(1)} %collective-permute-done.1.refs_2_, ...), custom_call_target="tpu_custom_call" | custom-call | tf_op jit(solution)/shard_map/pallas_call | solution.py:214
  19.0 0.1 collective-permute-start.3
  19.1 1.5 %collective-permute-done.3.got.near = bf16[2,72,768]{2,1,0:T(8,128)(2,1)S(1)} collective-permute-done((bf16[2,72,768]{2,1,0:T(8,128)(2,1)S(1)}, bf16[2,72,768]{2,1,0:T(8,128)(2,1)S(1)}, u32[]{:S(2)}, u32[]{:S(2)}) %collective-permute-start.3) | collective-permute-done | bytes 221216 | tf_op jit(solution)/shard_map/ppermute | solution.py:193
  20.6 0.0 copy-start.4
  20.6 0.0 copy-start.2
  20.6 0.0 copy-start
  20.6 0.2 shard_map.66
  20.7 1.5 %collective-permute-start.4 = (bf16[72,768]{1,0:T(8,128)(2,1)S(1)}, bf16[72,768]{1,0:T(8,128)(2,1)S(1)}, u32[]{:S(2)}, u32[]{:S(2)}) collective-permute-start(bf16[72,768]{1,0:T(8,128)(2,1)S(1)} %shard_map.66), channel_id=1, source_target_pairs={{0,2},{1,3},{2,0},{3,1},{4,6},{5,7},{6,4},{7,5},{8,10},{9,11},{10,... | collective-permute-start | bytes 331784 | tf_op jit(solution)/shard_map/ppermute | solution.py:193
  22.2 0.0 copy-done.4
  22.2 0.2 shard_map.67.long_ref
  22.4 3.4 %collective-permute-done.4.far = bf16[72,768]{1,0:T(8,128)(2,1)S(1)} collective-permute-done((bf16[72,768]{1,0:T(8,128)(2,1)S(1)}, bf16[72,768]{1,0:T(8,128)(2,1)S(1)}, u32[]{:S(2)}, u32[]{:S(2)}) %collective-permute-start.4) | collective-permute-done | bytes 110624 | tf_op jit(solution)/shard_map/ppermute | solution.py:193
  25.8 0.0 copy-done.2
  25.8 0.3 shard_map.68.refs_0_
  26.1 0.1 collective-permute-start.5
  26.2 1.5 %collective-permute-start.6 = (bf16[32,512]{1,0:T(8,128)(2,1)S(1)}, bf16[32,512]{1,0:T(8,128)(2,1)S(1)}, u32[]{:S(2)}, u32[]{:S(2)}) collective-permute-start(bf16[32,512]{1,0:T(8,128)(2,1)S(1)} %shard_map.68.refs_0_), channel_id=1, source_target_pairs={{0,8},{4,12},{8,0},{12,4},{1,9},{5,13},{9,1},{13,5},{2,10},{6,14},... | collective-permute-start | bytes 98312 | tf_op jit(solution)/shard_map/ppermute | solution.py:193
  27.7 2.8 %collective-permute-start.7 = (bf16[32,512]{1,0:T(8,128)(2,1)S(1)}, bf16[32,512]{1,0:T(8,128)(2,1)S(1)}, u32[]{:S(2)}, u32[]{:S(2)}) collective-permute-start(bf16[32,512]{1,0:T(8,128)(2,1)S(1)} %shard_map.68.refs_0_), channel_id=1, source_target_pairs={{0,12},{4,8},{8,4},{12,0},{1,13},{5,9},{9,5},{13,1},{2,14},{6,10},... | collective-permute-start | bytes 98312 | tf_op jit(solution)/shard_map/ppermute | solution.py:193
  30.6 0.0 collective-permute-done.5.refs_1_
  30.6 0.9 %collective-permute-done.6.refs_2_ = bf16[32,512]{1,0:T(8,128)(2,1)S(1)} collective-permute-done((bf16[32,512]{1,0:T(8,128)(2,1)S(1)}, bf16[32,512]{1,0:T(8,128)(2,1)S(1)}, u32[]{:S(2)}, u32[]{:S(2)}) %collective-permute-start.6) | collective-permute-done | bytes 32800 | tf_op jit(solution)/shard_map/ppermute | solution.py:193
  31.4 2.0 %collective-permute-done.7.refs_3_ = bf16[32,512]{1,0:T(8,128)(2,1)S(1)} collective-permute-done((bf16[32,512]{1,0:T(8,128)(2,1)S(1)}, bf16[32,512]{1,0:T(8,128)(2,1)S(1)}, u32[]{:S(2)}, u32[]{:S(2)}) %collective-permute-start.7) | collective-permute-done | bytes 32800 | tf_op jit(solution)/shard_map/ppermute | solution.py:193
  33.4 0.0 copy-done
  33.4 2.5 %shard_map.69 = (bf16[2,8,2048]{2,1,0:T(8,128)(2,1)S(1)}, f32[2,8,2048]{2,1,0:T(8,128)S(1)}) custom-call(bf16[32,512]{1,0:T(8,128)(2,1)S(1)} %shard_map.68.refs_0_, bf16[32,512]{1,0:T(8,128)(2,1)S(1)} %collective-permute-done.5.refs_1_, bf16[32,512]{1,0:T(8,128)(2,1)S(1)} %collective-permute-done.6.refs_2_, ...), custom_call_target="tpu_custom_call" | custom-call | tf_op jit(solution)/shard_map/pallas_call | solution.py:234
  35.9 0.1 collective-permute-start.8
  36.0 1.2 %collective-permute-done.8.got.near = bf16[2,8,2048]{2,1,0:T(8,128)(2,1)S(1)} collective-permute-done((bf16[2,8,2048]{2,1,0:T(8,128)(2,1)S(1)}, bf16[2,8,2048]{2,1,0:T(8,128)(2,1)S(1)}, u32[]{:S(2)}, u32[]{:S(2)}) %collective-permute-start.8) | collective-permute-done | bytes 65568 | tf_op jit(solution)/shard_map/ppermute | solution.py:193
  37.2 1.6 %collective-permute-start.9 = (bf16[8,2048]{1,0:T(8,128)(2,1)S(1)}, bf16[8,2048]{1,0:T(8,128)(2,1)S(1)}, u32[]{:S(2)}, u32[]{:S(2)}) collective-permute-start(bf16[8,2048]{1,0:T(8,128)(2,1)S(1)} %shard_map.70), channel_id=1, source_target_pairs={{0,2},{1,3},{2,0},{3,1},{4,6},{5,7},{6,4},{7,5},{8,10},{9,11},{10,... | collective-permute-start | bytes 98312 | tf_op jit(solution)/shard_map/ppermute | solution.py:193
  38.8 2.4 %collective-permute-done.9.far = bf16[8,2048]{1,0:T(8,128)(2,1)S(1)} collective-permute-done((bf16[8,2048]{1,0:T(8,128)(2,1)S(1)}, bf16[8,2048]{1,0:T(8,128)(2,1)S(1)}, u32[]{:S(2)}, u32[]{:S(2)}) %collective-permute-start.9) | collective-permute-done | bytes 32800 | tf_op jit(solution)/shard_map/ppermute | solution.py:193
  41.2 0.6 %shard_map.71 = bf16[8,2048]{1,0:T(8,128)(2,1)} custom-call(f32[2,8,2048]{2,1,0:T(8,128)S(1)} %get-tuple-element.11.keep, bf16[2,8,2048]{2,1,0:T(8,128)(2,1)S(1)} %collective-permute-done.8.got.near, bf16[8,2048]{1,0:T(8,128)(2,1)S(1)} %collective-permute-done.9.far), custom_call_target="tpu_custom_call" | custom-call | tf_op jit(solution)/shard_map/pallas_call | solution.py:244
  (2 shorter events, 0.0 us)
Async XLA Ops:
  0.0 12.3 %copy-start.3 = (f32[2048]{0:T(1024)S(1)}, f32[2048]{0:T(1024)}, u32[]{:S(2)}) copy-start(f32[2048]{0:T(1024)} %param.7) | copy-start | bytes 24580
  0.0 12.3 %copy-start.1 = (bf16[3,2048,2048]{2,1,0:T(8,128)(2,1)S(1)}, bf16[3,2048,2048]{2,1,0:T(8,128)(2,1)}, u32[]{:S(2)}) copy-start(bf16[3,2048,2048]{2,1,0:T(8,128)(2,1)} %refs_5_.1) | copy-start | bytes 75497472
  0.0 0.9 %copy-start.5 = (bf16[8,2048]{1,0:T(8,128)(2,1)S(1)}, bf16[8,2048]{1,0:T(8,128)(2,1)}, u32[]{:S(2)}) copy-start(bf16[8,2048]{1,0:T(8,128)(2,1)} %x_ref.1) | copy-start | bytes 98308
  0.9 5.6 %collective-permute-start = (bf16[8,2048]{1,0:T(8,128)(2,1)S(1)}, bf16[8,2048]{1,0:T(8,128)(2,1)S(1)}, u32[]{:S(2)}, u32[]{:S(2)}) collective-permute-start(bf16[8,2048]{1,0:T(8,128)(2,1)S(1)} %shard_map.64.refs_0_), channel_id=1, source_target_pairs={{0,4},{4,0},{8,12},{12,8},{1,5},{5,1},{9,13},{13,9},{2,6},{6,2},{1... | collective-permute-start | bytes 98312 | tf_op jit(solution)/shard_map/ppermute | solution.py:193
  4.0 5.4 %collective-permute-start.1 = (bf16[8,2048]{1,0:T(8,128)(2,1)S(1)}, bf16[8,2048]{1,0:T(8,128)(2,1)S(1)}, u32[]{:S(2)}, u32[]{:S(2)}) collective-permute-start(bf16[8,2048]{1,0:T(8,128)(2,1)S(1)} %shard_map.64.refs_0_), channel_id=1, source_target_pairs={{0,8},{4,12},{8,0},{12,4},{1,9},{5,13},{9,1},{13,5},{2,10},{6,14},... | collective-permute-start | bytes 98312 | tf_op jit(solution)/shard_map/ppermute | solution.py:193
  6.6 5.7 %collective-permute-start.2 = (bf16[8,2048]{1,0:T(8,128)(2,1)S(1)}, bf16[8,2048]{1,0:T(8,128)(2,1)S(1)}, u32[]{:S(2)}, u32[]{:S(2)}) collective-permute-start(bf16[8,2048]{1,0:T(8,128)(2,1)S(1)} %shard_map.64.refs_0_), channel_id=1, source_target_pairs={{0,12},{4,8},{8,4},{12,0},{1,13},{5,9},{9,5},{13,1},{2,14},{6,10},... | collective-permute-start | bytes 98312 | tf_op jit(solution)/shard_map/ppermute | solution.py:193
  19.0 1.5 %collective-permute-start.3 = (bf16[2,72,768]{2,1,0:T(8,128)(2,1)S(1)}, bf16[2,72,768]{2,1,0:T(8,128)(2,1)S(1)}, u32[]{:S(2)}, u32[]{:S(2)}) collective-permute-start(bf16[2,72,768]{2,1,0:T(8,128)(2,1)S(1)} %get-tuple-element.10), channel_id=1, source_target_pairs={{0,1},{1,0},{2,3},{3,2},{4,5},{5,4},{6,7},{7,6},{8,9},{9,8},{10,11... | collective-permute-start | bytes 663560 | tf_op jit(solution)/shard_map/ppermute | solution.py:193
  20.6 1.7 %copy-start.4 = (f32[7,128]{1,0:T(8,128)S(1)}, f32[7,128]{1,0:T(8,128)}, u32[]{:S(2)}) copy-start(f32[7,128]{1,0:T(8,128)} %se.1) | copy-start | bytes 10756
  20.6 5.3 %copy-start.2 = (f32[3,3,2048]{2,1,0:T(4,128)S(1)}, f32[3,3,2048]{2,1,0:T(4,128)}, u32[]{:S(2)}) copy-start(f32[3,3,2048]{2,1,0:T(4,128)} %short.1) | copy-start | bytes 221188
  20.6 12.9 %copy-start = (bf16[2048,8192]{1,0:T(8,128)(2,1)S(1)}, bf16[2048,8192]{1,0:T(8,128)(2,1)}, u32[]{:S(2)}) copy-start(bf16[2048,8192]{1,0:T(8,128)(2,1)} %refs_4_.1) | copy-start | bytes 100663296
  20.7 5.1 %collective-permute-start.4 = (bf16[72,768]{1,0:T(8,128)(2,1)S(1)}, bf16[72,768]{1,0:T(8,128)(2,1)S(1)}, u32[]{:S(2)}, u32[]{:S(2)}) collective-permute-start(bf16[72,768]{1,0:T(8,128)(2,1)S(1)} %shard_map.66), channel_id=1, source_target_pairs={{0,2},{1,3},{2,0},{3,1},{4,6},{5,7},{6,4},{7,5},{8,10},{9,11},{10,... | collective-permute-start | bytes 331784 | tf_op jit(solution)/shard_map/ppermute | solution.py:193
  26.1 4.5 %collective-permute-start.5 = (bf16[32,512]{1,0:T(8,128)(2,1)S(1)}, bf16[32,512]{1,0:T(8,128)(2,1)S(1)}, u32[]{:S(2)}, u32[]{:S(2)}) collective-permute-start(bf16[32,512]{1,0:T(8,128)(2,1)S(1)} %shard_map.68.refs_0_), channel_id=1, source_target_pairs={{0,4},{4,0},{8,12},{12,8},{1,5},{5,1},{9,13},{13,9},{2,6},{6,2},{1... | collective-permute-start | bytes 98312 | tf_op jit(solution)/shard_map/ppermute | solution.py:193
  26.2 5.2 %collective-permute-start.6 = (bf16[32,512]{1,0:T(8,128)(2,1)S(1)}, bf16[32,512]{1,0:T(8,128)(2,1)S(1)}, u32[]{:S(2)}, u32[]{:S(2)}) collective-permute-start(bf16[32,512]{1,0:T(8,128)(2,1)S(1)} %shard_map.68.refs_0_), channel_id=1, source_target_pairs={{0,8},{4,12},{8,0},{12,4},{1,9},{5,13},{9,1},{13,5},{2,10},{6,14},... | collective-permute-start | bytes 98312 | tf_op jit(solution)/shard_map/ppermute | solution.py:193
  27.7 5.7 %collective-permute-start.7 = (bf16[32,512]{1,0:T(8,128)(2,1)S(1)}, bf16[32,512]{1,0:T(8,128)(2,1)S(1)}, u32[]{:S(2)}, u32[]{:S(2)}) collective-permute-start(bf16[32,512]{1,0:T(8,128)(2,1)S(1)} %shard_map.68.refs_0_), channel_id=1, source_target_pairs={{0,12},{4,8},{8,4},{12,0},{1,13},{5,9},{9,5},{13,1},{2,14},{6,10},... | collective-permute-start | bytes 98312 | tf_op jit(solution)/shard_map/ppermute | solution.py:193
  35.9 1.3 %collective-permute-start.8 = (bf16[2,8,2048]{2,1,0:T(8,128)(2,1)S(1)}, bf16[2,8,2048]{2,1,0:T(8,128)(2,1)S(1)}, u32[]{:S(2)}, u32[]{:S(2)}) collective-permute-start(bf16[2,8,2048]{2,1,0:T(8,128)(2,1)S(1)} %get-tuple-element.12), channel_id=1, source_target_pairs={{0,1},{1,0},{2,3},{3,2},{4,5},{5,4},{6,7},{7,6},{8,9},{9,8},{10,11... | collective-permute-start | bytes 196616 | tf_op jit(solution)/shard_map/ppermute | solution.py:193
  37.2 4.0 %collective-permute-start.9 = (bf16[8,2048]{1,0:T(8,128)(2,1)S(1)}, bf16[8,2048]{1,0:T(8,128)(2,1)S(1)}, u32[]{:S(2)}, u32[]{:S(2)}) collective-permute-start(bf16[8,2048]{1,0:T(8,128)(2,1)S(1)} %shard_map.70), channel_id=1, source_target_pairs={{0,2},{1,3},{2,0},{3,1},{4,6},{5,7},{6,4},{7,5},{8,10},{9,11},{10,... | collective-permute-start | bytes 98312 | tf_op jit(solution)/shard_map/ppermute | solution.py:193

commit v2 on v1

--- a/solution.py
+++ b/solution.py
@@ -76,45 +76,63 @@
     )
 
 
-def project_body(seq, quarter, *refs):
-    pieces, (gain, w_in), (send, keep), (wide,) = refs[:seq], refs[seq : seq + 2], refs[seq + 2 : seq + 4], refs[seq + 4 :]
-    s, c = lax.axis_index("seq"), lax.axis_index("chan")
+def products(w_in, packs, chip, comp):
+    c = lax.axis_index("chan")
+    half = w_in.shape[1] // (2 * lax.axis_size("chan"))
+    total = None
+    for other in range(2):
+        owner = jnp.bitwise_xor(c, 2 * chip + other)
+        for h in range(2):
+            start = pl.multiple_of((2 * owner + h) * half, half)
+            term = contract_last(w_in[comp, pl.ds(start, half), :], packs[2 * other + h])
+            total = term if total is None else total + term
+    return total.T
+
+
+def put(flipped, comp, keep, send):
+    rows, half = flipped.shape[0] // 2, flipped.shape[1]
+    keep[:rows, comp * half : (comp + 1) * half] = flipped[:rows]
+    send[:rows, comp * half : (comp + 1) * half] = flipped[rows:].astype(send.dtype)
+
+
+def put_squares(packed, keep, send):
+    width = packed.shape[1]
+    for ref in (keep, send):
+        rows, columns = ref.shape
+        ref[rows - 8 :, :width] = packed.astype(ref.dtype)
+        ref[rows - 8 :, width:] = jnp.zeros((8, columns - width), ref.dtype)
+
+
+def first_body(seq, *refs):
+    pieces, (gain, w_in), (send, keep, scaled, packed), (wide,) = refs[:seq], refs[seq : seq + 2], refs[seq + 2 : seq + 6], refs[seq + 6 :]
+    s = lax.axis_index("seq")
     rows = pieces[0].shape[0]
     for hop in range(seq):
         place = pl.multiple_of(jnp.bitwise_xor(s, hop) * rows, rows)
         wide[pl.ds(place, rows), :] = pieces[hop][...].astype(F32)
     tokens = wide[...]
-    squares = jnp.sum(tokens * tokens, axis=1, keepdims=True)
-    packs = spread((tokens * gain[...]).astype(BF16))
-    count = tokens.shape[0]
-    half = quarter // 2
-    for other in (1, 0):
-        for comp in range(3):
-            total = None
-            for chip in range(2):
-                owner = jnp.bitwise_xor(c, 2 * chip + other)
-                for h in range(2):
-                    start = pl.multiple_of(owner * quarter + h * half, half)
-                    term = contract_last(w_in[comp, pl.ds(start, half), :], packs[2 * chip + h])
-                    total = term if total is None else total + term
-            flipped = total.T
-            for chip in range(2):
-                value = flipped[2 * chip * count : 2 * (chip + 1) * count]
-                if other:
-                    send[chip, : 2 * count, comp * half : (comp + 1) * half] = value.astype(BF16)
-                else:
-                    keep[chip, : 2 * count, comp * half : (comp + 1) * half] = value
-    packed = high_low(squares)
-    width = packed.shape[1]
-    for chip in range(2):
-        keep[chip, 2 * count :, :width] = packed
-        send[chip, 2 * count :, :width] = packed.astype(BF16)
-        keep[chip, 2 * count :, width:] = jnp.zeros((8, 3 * half - width), F32)
-        send[chip, 2 * count :, width:] = jnp.zeros((8, 3 * half - width), BF16)
-
-
-def relay_body(rows, keep, got, out):
-    value = keep[1] + got[1].astype(F32)
+    packed[...] = high_low(jnp.sum(tokens * tokens, axis=1, keepdims=True))
+    scaled[...] = (tokens * gain[...]).astype(BF16)
+    packs = spread(scaled[...])
+    for comp in range(3):
+        put(products(w_in, packs, 1, comp), comp, keep, send)
+    put_squares(packed[...], keep, send)
+
+
+def second_body(scaled, w_in, out):
+    out[...] = products(w_in, spread(scaled[...]), 0, 0)
+
+
+def third_body(scaled, w_in, packed, begun, _, send, keep):
+    put(begun[...], 0, keep, send)
+    packs = spread(scaled[...])
+    for comp in (1, 2):
+        put(products(w_in, packs, 0, comp), comp, keep, send)
+    put_squares(packed[...], keep, send)
+
+
+def relay_body(rows, keep, got, _, out):
+    value = keep[...] + got[...].astype(F32)
     out[:rows, :] = value[:rows].astype(BF16)
     count = rows // 16
     width = count * LANES
@@ -131,7 +149,7 @@
 
 def mix_body(features, keep, near, far, short, long_ref, out):
     c = lax.axis_index("chan")
-    value = keep[0] + near[0].astype(F32) + far[...].astype(F32)
+    value = keep[...] + near[...].astype(F32) + far[...].astype(F32)
     rows = value.shape[0] - 8
     count = rows // 2
     half = value.shape[1] // 3
@@ -152,20 +170,30 @@
         out[:, h * half : (h + 1) * half] = (featured[0] * filtered).astype(BF16)
 
 
-def output_body(seq, quarter, *refs):
-    pieces, w_out, (send, keep), (wide,) = refs[:seq], refs[seq], refs[seq + 1 : seq + 3], refs[seq + 3 :]
+def load_body(seq, quarter, w_out, w_part, sems):
+    c = lax.axis_index("chan")
+    copies = []
+    for source in range(seq):
+        start = pl.multiple_of(source * (w_out.shape[1] // seq) + c * quarter, LANES)
+        copies.append(pltpu.make_async_copy(w_out.at[:, pl.ds(start, quarter)], w_part.at[source], sems.at[source]))
+    for copy in copies:
+        copy.start()
+    for copy in copies:
+        copy.wait()
+
+
+def output_body(seq, *refs):
+    pieces, w_part, (send, keep), (wide,) = refs[:seq], refs[seq], refs[seq + 1 : seq + 3], refs[seq + 3 :]
     s, c = lax.axis_index("seq"), lax.axis_index("chan")
-    outputs = w_out.shape[0]
-    block = w_out.shape[1] // seq
+    outputs = w_part.shape[1]
     part = outputs // PACK
     count = pieces[0].shape[0]
     total = None
     for hop in range(seq):
         source = jnp.bitwise_xor(s, hop)
-        start = pl.multiple_of(source * block + c * quarter, LANES)
         packs = spread(pieces[hop][...])
         for q in range(PACK):
-            term = contract_last(w_out[q * part : (q + 1) * part, pl.ds(start, quarter)], packs[q])
+            term = contract_last(w_part[source, q * part : (q + 1) * part, :], packs[q])
             total = term if total is None else total + term
     flipped = total.T
     for q in range(PACK):
@@ -194,7 +222,10 @@
 
 
 def gathered(value, axis):
-    return [value] + [swap(value, axis, bit) for bit in range(1, lax.axis_size(axis))]
+    pieces = [value]
+    for bit in range(1, lax.axis_size(axis)):
+        pieces.append(swap(value, axis, bit))
+    return pieces
 
 
 def short_shards(x_tokens, norm_gain, w_in, short_filter, se_filter, w_out):
@@ -211,33 +242,41 @@
     pieces = gathered(x_tokens, "seq")
     held_in = pltpu.with_memory_space_constraint(w_in, pltpu.VMEM)
     long_taps = call(taps_body, struct((se_filter.shape[0], quarter), F32), [VMEM])(se_filter)
-    send, keep = call(
-        functools.partial(project_body, seq, quarter),
-        (
-            struct((2, wide_rows, wide_columns), BF16),
-            struct((2, wide_rows, wide_columns), F32),
-        ),
+    payload = struct((wide_rows, wide_columns), BF16), struct((wide_rows, wide_columns), F32)
+    send, keep, scaled, packed = call(
+        functools.partial(first_body, seq),
+        (*payload, struct((tokens, columns), BF16), struct((8, tokens // 8 * LANES), F32)),
         [VMEM] * (seq + 2),
         scratch=[pltpu.VMEM((tokens, columns), F32)],
         limit=10,
     )(*pieces, norm_gain.reshape(1, columns), held_in)
     near = swap(send, "chan", 1)
+    begun = call(second_body, struct((PACK * tokens, quarter // 2), F32), [VMEM] * 2, limit=3)(scaled, held_in)
     relay = call(
-        functools.partial(relay_body, 2 * tokens), struct((wide_rows, wide_columns), BF16), [VMEM] * 2, cost=ahead(w_out, 4)
-    )(keep, near)
+        functools.partial(relay_body, 2 * tokens), payload[0], [VMEM] * 3
+    )(keep, near, begun)
     far = swap(relay, "chan", 2)
+    send, keep = call(third_body, payload, [VMEM] * 5, limit=3)(scaled, held_in, packed, begun, relay)
+    near = swap(send, "chan", 1)
     gated = call(
         functools.partial(mix_body, columns * chan), struct((tokens, quarter), BF16), [VMEM] * 5
     )(keep, near, far, short_filter, long_taps)
     pieces = gathered(gated, "seq")
     outputs = w_out.shape[0]
+    w_part = call(
+        functools.partial(load_body, seq, quarter),
+        pltpu.VMEM((seq, outputs, quarter), BF16),
+        [ANY],
+        scratch=[pltpu.SemaphoreType.DMA((seq,))],
+        limit=1,
+    )(pltpu.with_memory_space_constraint(w_out, pltpu.HBM))
     send, keep = call(
-        functools.partial(output_body, seq, quarter),
+        functools.partial(output_body, seq),
         (struct((2, tokens // chan, outputs), BF16), struct((2, tokens // chan, outputs), F32)),
         [VMEM] * (seq + 1),
         scratch=[pltpu.VMEM((tokens, outputs), F32)],
         limit=6,
-    )(*pieces, pltpu.with_memory_space_constraint(w_out, pltpu.VMEM))
+    )(*pieces, w_part)
     near = swap(send, "chan", 1)
     relay = call(pass_body, struct((tokens // chan, outputs), BF16), [VMEM] * 2)(keep, near)
     far = swap(relay, "chan", 2)

time: 42 us -> 40.8 us (0.971)
  waiting for transfers between devices: 17.1 us -> 11.3 us
  Pallas kernels: 10.4 us -> 14.5 us
  starting transfers between devices: 13.3 us -> 13.8 us
    ppermute x10 -> x11, waiting for transfers between devices: 17.1 us -> 11.3 us  [swap(): lax.ppermute(value, axis, [(i, i ^ bit) for i in range(lax.axis_size(axis...]
    pallas_call x3 -> x6, Pallas kernels: 9.35 us -> 13.4 us  [the longest x1 3.55 us: short_shards(): call(functools.partial(load_body, seq, quarter), pltpu.VMEM((seq, outputs...]
    ppermute x10 -> x11, starting transfers between devices: 13.3 us -> 13.8 us  [swap(): lax.ppermute(value, axis, [(i, i ^ bit) for i in range(lax.axis_size(axis...]
    unnamed x12 -> x10, local copies, waits for them, and re-layouts: 0.93 us -> 0.93 us
  transfers between devices with their start and end apart: 10 -> 11, of which waited for: 8 -> 5; matrix products, arithmetic and copies ran while one was open for 0% -> 0% of each run, Pallas kernels for 0% -> 12%
where the time goes in v2:
time: 40.8 us; the launch traced here: 40.7 us
  Pallas kernels  14.5 us (36%)
  starting transfers between devices  13.8 us (34%)
  waiting for transfers between devices  11.3 us (28%)
  local copies, waits for them, and re-layouts  0.93 us (2%)
    ppermute x11, starting transfers between devices, swap(): lax.ppermute(value, axis, [(i, i ^ bit) for i in range(lax.axis_size(axis...  13.8 us
    ppermute x11, waiting for transfers between devices, swap(): lax.ppermute(value, axis, [(i, i ^ bit) for i in range(lax.axis_size(axis...  11.3 us
    pallas_call x1, Pallas kernels, short_shards(): call(functools.partial(load_body, seq, quarter), pltpu.VMEM((seq, outputs...  3.55 us
    pallas_call x1, Pallas kernels, short_shards(): call(functools.partial(first_body, seq), (*payload, struct((tokens, colum...  3.51 us
    pallas_call x1, Pallas kernels, short_shards(): call(functools.partial(output_body, seq), (struct((2, tokens // chan, out...  2.45 us
    pallas_call x1, Pallas kernels, short_shards(): call(third_body, payload, [VMEM] * 5, limit=3)  2.41 us
    pallas_call x1, Pallas kernels, short_shards(): call(second_body, struct((PACK * tokens, quarter // 2), F32), [VMEM] * 2,...  1.31 us
    unnamed x10, local copies, waits for them, and re-layouts  0.93 us
  transfers between devices with their start and end apart: 11, of which 5 were waited for; matrix products, arithmetic and copies ran while one was open for 0% of the time, Pallas kernels for 12%

profile of v2, /device:TPU:0, one launch (start us, length us, event | category | flops | bytes accessed | tf_op | source)
XLA Modules:
  0.0 40.7 jit_solution(2022401280226748754)
XLA Ops:
  0.0 0.0 copy-start
  0.0 0.0 copy-start.2
  0.0 0.0 copy-start.4
  0.0 0.9 %copy-done.4 = bf16[8,2048]{1,0:T(8,128)(2,1)S(1)} copy-done((bf16[8,2048]{1,0:T(8,128)(2,1)S(1)}, bf16[8,2048]{1,0:T(8,128)(2,1)}, u32[]{:S(2)}) %copy-start.4) | copy-done | bytes 32792
  0.9 5.1 %collective-permute-start.2 = (bf16[8,2048]{1,0:T(8,128)(2,1)S(1)}, bf16[8,2048]{1,0:T(8,128)(2,1)S(1)}, u32[]{:S(2)}, u32[]{:S(2)}) collective-permute-start(bf16[8,2048]{1,0:T(8,128)(2,1)S(1)} %shard_map.64.refs_0_), channel_id=1, source_target_pairs={{0,12},{4,8},{8,4},{12,0},{1,13},{5,9},{9,5},{13,1},{2,14},{6,10},... | collective-permute-start | bytes 98312 | tf_op jit(solution)/shard_map/ppermute | solution.py:221
  6.0 0.0 collective-permute-start.1
  6.0 0.6 %collective-permute-start = (bf16[8,2048]{1,0:T(8,128)(2,1)S(1)}, bf16[8,2048]{1,0:T(8,128)(2,1)S(1)}, u32[]{:S(2)}, u32[]{:S(2)}) collective-permute-start(bf16[8,2048]{1,0:T(8,128)(2,1)S(1)} %shard_map.64.refs_0_), channel_id=1, source_target_pairs={{0,4},{4,0},{8,12},{12,8},{1,5},{5,1},{9,13},{13,9},{2,6},{6,2},{1... | collective-permute-start | bytes 98312 | tf_op jit(solution)/shard_map/ppermute | solution.py:221
  6.6 1.3 %collective-permute-done.2.refs_3_ = bf16[8,2048]{1,0:T(8,128)(2,1)S(1)} collective-permute-done((bf16[8,2048]{1,0:T(8,128)(2,1)S(1)}, bf16[8,2048]{1,0:T(8,128)(2,1)S(1)}, u32[]{:S(2)}, u32[]{:S(2)}) %collective-permute-start.2) | collective-permute-done | bytes 32800 | tf_op jit(solution)/shard_map/ppermute | solution.py:221
  7.9 2.9 %collective-permute-done.1.refs_2_ = bf16[8,2048]{1,0:T(8,128)(2,1)S(1)} collective-permute-done((bf16[8,2048]{1,0:T(8,128)(2,1)S(1)}, bf16[8,2048]{1,0:T(8,128)(2,1)S(1)}, u32[]{:S(2)}, u32[]{:S(2)}) %collective-permute-start.1) | collective-permute-done | bytes 32800 | tf_op jit(solution)/shard_map/ppermute | solution.py:221
  10.8 0.0 collective-permute-done.refs_1_
  10.8 0.0 copy-done
  10.8 0.0 copy-done.2
  10.8 3.5 %shard_map.65 = (bf16[72,768]{1,0:T(8,128)(2,1)S(1)}, f32[72,768]{1,0:T(8,128)S(1)}, bf16[32,2048]{1,0:T(8,128)(2,1)S(1)}, f32[8,512]{1,0:T(8,128)S(1)}) custom-call(bf16[8,2048]{1,0:T(8,128)(2,1)S(1)} %shard_map.64.refs_0_, bf16[8,2048]{1,0:T(8,128)(2,1)S(1)} %collective-permute-done.refs_1_, bf16[8,2048]{1,0:T(8,128)(2,1)S(1)} %collective-permute-done.1.refs_2_, ...), custom_call_target="tpu_custom_call" | custom-call | tf_op jit(solution)/shard_map/pallas_call | solution.py:246
  14.3 0.1 collective-permute-start.3
  14.4 0.0 copy-start.3
  14.4 0.0 copy-start.1
  14.4 1.3 %shard_map.66._.begun = f32[128,256]{1,0:T(8,128)S(1)} custom-call(bf16[32,2048]{1,0:T(8,128)(2,1)S(1)} %get-tuple-element.13.scaled, bf16[3,2048,2048]{2,1,0:T(8,128)(2,1)S(1)} %copy-done), custom_call_target="tpu_custom_call" | custom-call | tf_op jit(solution)/shard_map/pallas_call | solution.py:254
  15.8 0.0 collective-permute-done.3.got
  15.8 0.2 shard_map.67._
  15.9 2.4 %shard_map.68 = (bf16[72,768]{1,0:T(8,128)(2,1)S(1)}, f32[72,768]{1,0:T(8,128)S(1)}) custom-call(bf16[32,2048]{1,0:T(8,128)(2,1)S(1)} %get-tuple-element.13.scaled, bf16[3,2048,2048]{2,1,0:T(8,128)(2,1)S(1)} %copy-done, f32[8,512]{1,0:T(8,128)S(1)} %get-tuple-element.14.packed, f32[128,256]{1,0:T(8,128)S(1)} %shard_map.66._.begun, ...), custom_call_target="tpu_custom_call" | custom-call | tf_op jit(solution)/shard_map/pallas_call | solution.py:259
  18.3 0.5 %collective-permute-start.4 = (bf16[72,768]{1,0:T(8,128)(2,1)S(1)}, bf16[72,768]{1,0:T(8,128)(2,1)S(1)}, u32[]{:S(2)}, u32[]{:S(2)}) collective-permute-start(bf16[72,768]{1,0:T(8,128)(2,1)S(1)} %get-tuple-element.18), channel_id=1, source_target_pairs={{0,1},{1,0},{2,3},{3,2},{4,5},{5,4},{6,7},{7,6},{8,9},{9,8},{10,11... | collective-permute-start | bytes 331784 | tf_op jit(solution)/shard_map/ppermute | solution.py:221
  18.9 1.5 %collective-permute-start.5 = (bf16[72,768]{1,0:T(8,128)(2,1)S(1)}, bf16[72,768]{1,0:T(8,128)(2,1)S(1)}, u32[]{:S(2)}, u32[]{:S(2)}) collective-permute-start(bf16[72,768]{1,0:T(8,128)(2,1)S(1)} %shard_map.67._), channel_id=1, source_target_pairs={{0,2},{1,3},{2,0},{3,1},{4,6},{5,7},{6,4},{7,5},{8,10},{9,11},{10,... | collective-permute-start | bytes 331784 | tf_op jit(solution)/shard_map/ppermute | solution.py:221
  20.4 0.0 copy-done.3
  20.4 0.2 shard_map.69.long_ref
  20.5 0.0 collective-permute-done.4.near
  20.6 3.4 %collective-permute-done.5.far = bf16[72,768]{1,0:T(8,128)(2,1)S(1)} collective-permute-done((bf16[72,768]{1,0:T(8,128)(2,1)S(1)}, bf16[72,768]{1,0:T(8,128)(2,1)S(1)}, u32[]{:S(2)}, u32[]{:S(2)}) %collective-permute-start.5) | collective-permute-done | bytes 110624 | tf_op jit(solution)/shard_map/ppermute | solution.py:221
  23.9 0.0 copy-done.1
  23.9 0.3 shard_map.70.refs_0_
  24.2 2.5 %collective-permute-start.8 = (bf16[32,512]{1,0:T(8,128)(2,1)S(1)}, bf16[32,512]{1,0:T(8,128)(2,1)S(1)}, u32[]{:S(2)}, u32[]{:S(2)}) collective-permute-start(bf16[32,512]{1,0:T(8,128)(2,1)S(1)} %shard_map.70.refs_0_), channel_id=1, source_target_pairs={{0,12},{4,8},{8,4},{12,0},{1,13},{5,9},{9,5},{13,1},{2,14},{6,10},... | collective-permute-start | bytes 98312 | tf_op jit(solution)/shard_map/ppermute | solution.py:221
  26.7 0.0 collective-permute-start.7
  26.7 2.0 %collective-permute-start.6 = (bf16[32,512]{1,0:T(8,128)(2,1)S(1)}, bf16[32,512]{1,0:T(8,128)(2,1)S(1)}, u32[]{:S(2)}, u32[]{:S(2)}) collective-permute-start(bf16[32,512]{1,0:T(8,128)(2,1)S(1)} %shard_map.70.refs_0_), channel_id=1, source_target_pairs={{0,4},{4,0},{8,12},{12,8},{1,5},{5,1},{9,13},{13,9},{2,6},{6,2},{1... | collective-permute-start | bytes 98312 | tf_op jit(solution)/shard_map/ppermute | solution.py:221
  28.7 3.5 %shard_map.71.refs_4_ = bf16[4,2048,512]{2,1,0:T(8,128)(2,1)S(1)} custom-call(bf16[2048,8192]{1,0:T(8,128)(2,1)} %w_out.1), custom_call_target="tpu_custom_call" | custom-call | tf_op jit(solution)/shard_map/pallas_call | solution.py:266
  32.2 0.0 collective-permute-done.8.refs_3_
  32.2 0.0 collective-permute-done.7.refs_2_
  32.2 0.0 collective-permute-done.6.refs_1_
  32.3 2.5 %shard_map.72 = (bf16[2,8,2048]{2,1,0:T(8,128)(2,1)S(1)}, f32[2,8,2048]{2,1,0:T(8,128)S(1)}) custom-call(bf16[32,512]{1,0:T(8,128)(2,1)S(1)} %shard_map.70.refs_0_, bf16[32,512]{1,0:T(8,128)(2,1)S(1)} %collective-permute-done.6.refs_1_, bf16[32,512]{1,0:T(8,128)(2,1)S(1)} %collective-permute-done.7.refs_2_, ...), custom_call_target="tpu_custom_call" | custom-call | tf_op jit(solution)/shard_map/pallas_call | solution.py:273
  34.7 0.1 collective-permute-start.9
  34.8 1.2 %collective-permute-done.9.got.near = bf16[2,8,2048]{2,1,0:T(8,128)(2,1)S(1)} collective-permute-done((bf16[2,8,2048]{2,1,0:T(8,128)(2,1)S(1)}, bf16[2,8,2048]{2,1,0:T(8,128)(2,1)S(1)}, u32[]{:S(2)}, u32[]{:S(2)}) %collective-permute-start.9) | collective-permute-done | bytes 65568 | tf_op jit(solution)/shard_map/ppermute | solution.py:221
  36.0 1.6 %collective-permute-start.10 = (bf16[8,2048]{1,0:T(8,128)(2,1)S(1)}, bf16[8,2048]{1,0:T(8,128)(2,1)S(1)}, u32[]{:S(2)}, u32[]{:S(2)}) collective-permute-start(bf16[8,2048]{1,0:T(8,128)(2,1)S(1)} %shard_map.73), channel_id=1, source_target_pairs={{0,2},{1,3},{2,0},{3,1},{4,6},{5,7},{6,4},{7,5},{8,10},{9,11},{10,... | collective-permute-start | bytes 98312 | tf_op jit(solution)/shard_map/ppermute | solution.py:221
  37.6 2.4 %collective-permute-done.10.far = bf16[8,2048]{1,0:T(8,128)(2,1)S(1)} collective-permute-done((bf16[8,2048]{1,0:T(8,128)(2,1)S(1)}, bf16[8,2048]{1,0:T(8,128)(2,1)S(1)}, u32[]{:S(2)}, u32[]{:S(2)}) %collective-permute-start.10) | collective-permute-done | bytes 32800 | tf_op jit(solution)/shard_map/ppermute | solution.py:221
  40.0 0.6 %shard_map.74 = bf16[8,2048]{1,0:T(8,128)(2,1)} custom-call(f32[2,8,2048]{2,1,0:T(8,128)S(1)} %get-tuple-element.19.keep, bf16[2,8,2048]{2,1,0:T(8,128)(2,1)S(1)} %collective-permute-done.9.got.near, bf16[8,2048]{1,0:T(8,128)(2,1)S(1)} %collective-permute-done.10.far), custom_call_target="tpu_custom_call" | custom-call | tf_op jit(solution)/shard_map/pallas_call | solution.py:283
  (2 shorter events, 0.0 us)
Async XLA Ops:
  0.0 10.8 %copy-start = (bf16[3,2048,2048]{2,1,0:T(8,128)(2,1)S(1)}, bf16[3,2048,2048]{2,1,0:T(8,128)(2,1)}, u32[]{:S(2)}) copy-start(bf16[3,2048,2048]{2,1,0:T(8,128)(2,1)} %w_in.3) | copy-start | bytes 75497472
  0.0 10.8 %copy-start.2 = (f32[2048]{0:T(1024)S(1)}, f32[2048]{0:T(1024)}, u32[]{:S(2)}) copy-start(f32[2048]{0:T(1024)} %param.7) | copy-start | bytes 24580
  0.0 0.9 %copy-start.4 = (bf16[8,2048]{1,0:T(8,128)(2,1)S(1)}, bf16[8,2048]{1,0:T(8,128)(2,1)}, u32[]{:S(2)}) copy-start(bf16[8,2048]{1,0:T(8,128)(2,1)} %x_ref.1) | copy-start | bytes 98308
  0.9 7.0 %collective-permute-start.2 = (bf16[8,2048]{1,0:T(8,128)(2,1)S(1)}, bf16[8,2048]{1,0:T(8,128)(2,1)S(1)}, u32[]{:S(2)}, u32[]{:S(2)}) collective-permute-start(bf16[8,2048]{1,0:T(8,128)(2,1)S(1)} %shard_map.64.refs_0_), channel_id=1, source_target_pairs={{0,12},{4,8},{8,4},{12,0},{1,13},{5,9},{9,5},{13,1},{2,14},{6,10},... | collective-permute-start | bytes 98312 | tf_op jit(solution)/shard_map/ppermute | solution.py:221
  6.0 4.8 %collective-permute-start.1 = (bf16[8,2048]{1,0:T(8,128)(2,1)S(1)}, bf16[8,2048]{1,0:T(8,128)(2,1)S(1)}, u32[]{:S(2)}, u32[]{:S(2)}) collective-permute-start(bf16[8,2048]{1,0:T(8,128)(2,1)S(1)} %shard_map.64.refs_0_), channel_id=1, source_target_pairs={{0,8},{4,12},{8,0},{12,4},{1,9},{5,13},{9,1},{13,5},{2,10},{6,14},... | collective-permute-start | bytes 98312 | tf_op jit(solution)/shard_map/ppermute | solution.py:221
  6.0 4.8 %collective-permute-start = (bf16[8,2048]{1,0:T(8,128)(2,1)S(1)}, bf16[8,2048]{1,0:T(8,128)(2,1)S(1)}, u32[]{:S(2)}, u32[]{:S(2)}) collective-permute-start(bf16[8,2048]{1,0:T(8,128)(2,1)S(1)} %shard_map.64.refs_0_), channel_id=1, source_target_pairs={{0,4},{4,0},{8,12},{12,8},{1,5},{5,1},{9,13},{13,9},{2,6},{6,2},{1... | collective-permute-start | bytes 98312 | tf_op jit(solution)/shard_map/ppermute | solution.py:221
  14.3 1.4 %collective-permute-start.3 = (bf16[72,768]{1,0:T(8,128)(2,1)S(1)}, bf16[72,768]{1,0:T(8,128)(2,1)S(1)}, u32[]{:S(2)}, u32[]{:S(2)}) collective-permute-start(bf16[72,768]{1,0:T(8,128)(2,1)S(1)} %get-tuple-element.16), channel_id=1, source_target_pairs={{0,1},{1,0},{2,3},{3,2},{4,5},{5,4},{6,7},{7,6},{8,9},{9,8},{10,11... | collective-permute-start | bytes 331784 | tf_op jit(solution)/shard_map/ppermute | solution.py:221
  14.4 6.0 %copy-start.3 = (f32[7,128]{1,0:T(8,128)S(1)}, f32[7,128]{1,0:T(8,128)}, u32[]{:S(2)}) copy-start(f32[7,128]{1,0:T(8,128)} %se.1) | copy-start | bytes 10756
  14.4 9.5 %copy-start.1 = (f32[3,3,2048]{2,1,0:T(4,128)S(1)}, f32[3,3,2048]{2,1,0:T(4,128)}, u32[]{:S(2)}) copy-start(f32[3,3,2048]{2,1,0:T(4,128)} %short.1) | copy-start | bytes 221188
  18.3 2.2 %collective-permute-start.4 = (bf16[72,768]{1,0:T(8,128)(2,1)S(1)}, bf16[72,768]{1,0:T(8,128)(2,1)S(1)}, u32[]{:S(2)}, u32[]{:S(2)}) collective-permute-start(bf16[72,768]{1,0:T(8,128)(2,1)S(1)} %get-tuple-element.18), channel_id=1, source_target_pairs={{0,1},{1,0},{2,3},{3,2},{4,5},{5,4},{6,7},{7,6},{8,9},{9,8},{10,11... | collective-permute-start | bytes 331784 | tf_op jit(solution)/shard_map/ppermute | solution.py:221
  18.9 5.0 %collective-permute-start.5 = (bf16[72,768]{1,0:T(8,128)(2,1)S(1)}, bf16[72,768]{1,0:T(8,128)(2,1)S(1)}, u32[]{:S(2)}, u32[]{:S(2)}) collective-permute-start(bf16[72,768]{1,0:T(8,128)(2,1)S(1)} %shard_map.67._), channel_id=1, source_target_pairs={{0,2},{1,3},{2,0},{3,1},{4,6},{5,7},{6,4},{7,5},{8,10},{9,11},{10,... | collective-permute-start | bytes 331784 | tf_op jit(solution)/shard_map/ppermute | solution.py:221
  24.2 8.0 %collective-permute-start.8 = (bf16[32,512]{1,0:T(8,128)(2,1)S(1)}, bf16[32,512]{1,0:T(8,128)(2,1)S(1)}, u32[]{:S(2)}, u32[]{:S(2)}) collective-permute-start(bf16[32,512]{1,0:T(8,128)(2,1)S(1)} %shard_map.70.refs_0_), channel_id=1, source_target_pairs={{0,12},{4,8},{8,4},{12,0},{1,13},{5,9},{9,5},{13,1},{2,14},{6,10},... | collective-permute-start | bytes 98312 | tf_op jit(solution)/shard_map/ppermute | solution.py:221
  26.7 5.5 %collective-permute-start.7 = (bf16[32,512]{1,0:T(8,128)(2,1)S(1)}, bf16[32,512]{1,0:T(8,128)(2,1)S(1)}, u32[]{:S(2)}, u32[]{:S(2)}) collective-permute-start(bf16[32,512]{1,0:T(8,128)(2,1)S(1)} %shard_map.70.refs_0_), channel_id=1, source_target_pairs={{0,8},{4,12},{8,0},{12,4},{1,9},{5,13},{9,1},{13,5},{2,10},{6,14},... | collective-permute-start | bytes 98312 | tf_op jit(solution)/shard_map/ppermute | solution.py:221
  26.7 5.5 %collective-permute-start.6 = (bf16[32,512]{1,0:T(8,128)(2,1)S(1)}, bf16[32,512]{1,0:T(8,128)(2,1)S(1)}, u32[]{:S(2)}, u32[]{:S(2)}) collective-permute-start(bf16[32,512]{1,0:T(8,128)(2,1)S(1)} %shard_map.70.refs_0_), channel_id=1, source_target_pairs={{0,4},{4,0},{8,12},{12,8},{1,5},{5,1},{9,13},{13,9},{2,6},{6,2},{1... | collective-permute-start | bytes 98312 | tf_op jit(solution)/shard_map/ppermute | solution.py:221
  34.7 1.3 %collective-permute-start.9 = (bf16[2,8,2048]{2,1,0:T(8,128)(2,1)S(1)}, bf16[2,8,2048]{2,1,0:T(8,128)(2,1)S(1)}, u32[]{:S(2)}, u32[]{:S(2)}) collective-permute-start(bf16[2,8,2048]{2,1,0:T(8,128)(2,1)S(1)} %get-tuple-element.20), channel_id=1, source_target_pairs={{0,1},{1,0},{2,3},{3,2},{4,5},{5,4},{6,7},{7,6},{8,9},{9,8},{10,11... | collective-permute-start | bytes 196616 | tf_op jit(solution)/shard_map/ppermute | solution.py:221
  36.0 4.0 %collective-permute-start.10 = (bf16[8,2048]{1,0:T(8,128)(2,1)S(1)}, bf16[8,2048]{1,0:T(8,128)(2,1)S(1)}, u32[]{:S(2)}, u32[]{:S(2)}) collective-permute-start(bf16[8,2048]{1,0:T(8,128)(2,1)S(1)} %shard_map.73), channel_id=1, source_target_pairs={{0,2},{1,3},{2,0},{3,1},{4,6},{5,7},{6,4},{7,5},{8,10},{9,11},{10,... | collective-permute-start | bytes 98312 | tf_op jit(solution)/shard_map/ppermute | solution.py:221

commit v3 on v2

--- a/solution.py
+++ b/solution.py
@@ -10,6 +10,7 @@
 GROUP = 16
 epsilon = 1e-06
 LANES = 128
+SPLIT = 1
 PACK = 4
 VMEM = pl.BlockSpec(memory_space=pltpu.VMEM)
 ANY = pl.BlockSpec(memory_space=pl.ANY)
@@ -170,30 +171,30 @@
         out[:, h * half : (h + 1) * half] = (featured[0] * filtered).astype(BF16)
 
 
-def load_body(seq, quarter, w_out, w_part, sems):
-    c = lax.axis_index("chan")
+def load_body(seq, quarter, hops, w_out, w_part, sems):
+    s, c = lax.axis_index("seq"), lax.axis_index("chan")
     copies = []
-    for source in range(seq):
-        start = pl.multiple_of(source * (w_out.shape[1] // seq) + c * quarter, LANES)
-        copies.append(pltpu.make_async_copy(w_out.at[:, pl.ds(start, quarter)], w_part.at[source], sems.at[source]))
+    for i, hop in enumerate(hops):
+        start = pl.multiple_of(jnp.bitwise_xor(s, hop) * (w_out.shape[1] // seq) + c * quarter, LANES)
+        copies.append(pltpu.make_async_copy(w_out.at[:, pl.ds(start, quarter)], w_part.at[i], sems.at[i]))
     for copy in copies:
         copy.start()
     for copy in copies:
         copy.wait()
 
 
-def output_body(seq, *refs):
-    pieces, w_part, (send, keep), (wide,) = refs[:seq], refs[seq], refs[seq + 1 : seq + 3], refs[seq + 3 :]
-    s, c = lax.axis_index("seq"), lax.axis_index("chan")
-    outputs = w_part.shape[1]
+def output_body(seq, split, *refs):
+    pieces, parts, (send, keep), (wide,) = refs[:seq], refs[seq : seq + 2], refs[seq + 2 : seq + 4], refs[seq + 4 :]
+    c = lax.axis_index("chan")
+    outputs = parts[0].shape[1]
     part = outputs // PACK
     count = pieces[0].shape[0]
     total = None
     for hop in range(seq):
-        source = jnp.bitwise_xor(s, hop)
+        columns = parts[0].at[hop] if hop < split else parts[1].at[hop - split]
         packs = spread(pieces[hop][...])
         for q in range(PACK):
-            term = contract_last(w_part[source, q * part : (q + 1) * part, :], packs[q])
+            term = contract_last(columns[q * part : (q + 1) * part, :], packs[q])
             total = term if total is None else total + term
     flipped = total.T
     for q in range(PACK):
@@ -242,7 +243,7 @@
     pieces = gathered(x_tokens, "seq")
     held_in = pltpu.with_memory_space_constraint(w_in, pltpu.VMEM)
     long_taps = call(taps_body, struct((se_filter.shape[0], quarter), F32), [VMEM])(se_filter)
-    payload = struct((wide_rows, wide_columns), BF16), struct((wide_rows, wide_columns), F32)
+    payload = (struct((wide_rows, wide_columns), F32),) * 2
     send, keep, scaled, packed = call(
         functools.partial(first_body, seq),
         (*payload, struct((tokens, columns), BF16), struct((8, tokens // 8 * LANES), F32)),
@@ -253,30 +254,32 @@
     near = swap(send, "chan", 1)
     begun = call(second_body, struct((PACK * tokens, quarter // 2), F32), [VMEM] * 2, limit=3)(scaled, held_in)
     relay = call(
-        functools.partial(relay_body, 2 * tokens), payload[0], [VMEM] * 3
+        functools.partial(relay_body, 2 * tokens), struct((wide_rows, wide_columns), BF16), [VMEM] * 3
     )(keep, near, begun)
     far = swap(relay, "chan", 2)
     send, keep = call(third_body, payload, [VMEM] * 5, limit=3)(scaled, held_in, packed, begun, relay)
     near = swap(send, "chan", 1)
+    outputs, w_parts = w_out.shape[0], []
+    for hops in (range(SPLIT), range(SPLIT, seq)):
+        loaded = call(
+            functools.partial(load_body, seq, quarter, hops),
+            pltpu.VMEM((len(hops), outputs, quarter), BF16),
+            [ANY],
+            scratch=[pltpu.SemaphoreType.DMA((len(hops),))],
+            limit=1,
+        )(pltpu.with_memory_space_constraint(w_out, pltpu.HBM))
+        w_parts.append(loaded)
     gated = call(
         functools.partial(mix_body, columns * chan), struct((tokens, quarter), BF16), [VMEM] * 5
     )(keep, near, far, short_filter, long_taps)
     pieces = gathered(gated, "seq")
-    outputs = w_out.shape[0]
-    w_part = call(
-        functools.partial(load_body, seq, quarter),
-        pltpu.VMEM((seq, outputs, quarter), BF16),
-        [ANY],
-        scratch=[pltpu.SemaphoreType.DMA((seq,))],
-        limit=1,
-    )(pltpu.with_memory_space_constraint(w_out, pltpu.HBM))
     send, keep = call(
-        functools.partial(output_body, seq),
+        functools.partial(output_body, seq, SPLIT),
         (struct((2, tokens // chan, outputs), BF16), struct((2, tokens // chan, outputs), F32)),
-        [VMEM] * (seq + 1),
+        [VMEM] * (seq + 2),
         scratch=[pltpu.VMEM((tokens, outputs), F32)],
         limit=6,
-    )(*pieces, w_part)
+    )(*pieces, *w_parts)
     near = swap(send, "chan", 1)
     relay = call(pass_body, struct((tokens // chan, outputs), BF16), [VMEM] * 2)(keep, near)
     far = swap(relay, "chan", 2)

time: 40.8 us -> 41.8 us (1.025)
  Pallas kernels: 14.5 us -> 15.4 us
    pallas_call x3 -> x4, Pallas kernels: 6.16 us -> 7.12 us  [the longest x2 4.53 us: short_shards(): call(functools.partial(load_body, seq, quarter, hops), pltpu.VMEM((len(ho...]
  transfers between devices with their start and end apart: 11 -> 11, of which waited for: 5 -> 6; matrix products, arithmetic and copies ran while one was open for 0% -> 0% of each run, Pallas kernels for 12% -> 14%
where the time goes in v3:
time: 41.8 us; the launch traced here: 41.7 us
  Pallas kernels  15.4 us (37%)
  starting transfers between devices  13.7 us (33%)
  waiting for transfers between devices  11.5 us (28%)
  local copies, waits for them, and re-layouts  0.93 us (2%)
    ppermute x11, starting transfers between devices, swap(): lax.ppermute(value, axis, [(i, i ^ bit) for i in range(lax.axis_size(axis...  13.7 us
    ppermute x11, waiting for transfers between devices, swap(): lax.ppermute(value, axis, [(i, i ^ bit) for i in range(lax.axis_size(axis...  11.5 us
    pallas_call x2, Pallas kernels, short_shards(): call(functools.partial(load_body, seq, quarter, hops), pltpu.VMEM((len(ho...  4.53 us
    pallas_call x1, Pallas kernels, short_shards(): call(functools.partial(first_body, seq), (*payload, struct((tokens, colum...  3.51 us
    pallas_call x1, Pallas kernels, short_shards(): call(functools.partial(output_body, seq, SPLIT), (struct((2, tokens // ch...  2.45 us
    pallas_call x1, Pallas kernels, short_shards(): call(third_body, payload, [VMEM] * 5, limit=3)  2.4 us
    pallas_call x1, Pallas kernels, short_shards(): call(second_body, struct((PACK * tokens, quarter // 2), F32), [VMEM] * 2,...  1.31 us
    unnamed x10, local copies, waits for them, and re-layouts  0.93 us
  transfers between devices with their start and end apart: 11, of which 6 were waited for; matrix products, arithmetic and copies ran while one was open for 0% of the time, Pallas kernels for 14%

profile of v3, /device:TPU:0, one launch (start us, length us, event | category | flops | bytes accessed | tf_op | source)
XLA Modules:
  0.0 41.7 jit_solution(10653389126926896915)
XLA Ops:
  0.0 0.0 copy-start
  0.0 0.0 copy-start.2
  0.0 0.0 copy-start.4
  0.0 0.9 %copy-done.4 = bf16[8,2048]{1,0:T(8,128)(2,1)S(1)} copy-done((bf16[8,2048]{1,0:T(8,128)(2,1)S(1)}, bf16[8,2048]{1,0:T(8,128)(2,1)}, u32[]{:S(2)}) %copy-start.4) | copy-done | bytes 32792
  0.9 5.1 %collective-permute-start.2 = (bf16[8,2048]{1,0:T(8,128)(2,1)S(1)}, bf16[8,2048]{1,0:T(8,128)(2,1)S(1)}, u32[]{:S(2)}, u32[]{:S(2)}) collective-permute-start(bf16[8,2048]{1,0:T(8,128)(2,1)S(1)} %shard_map.64.refs_0_), channel_id=1, source_target_pairs={{0,12},{4,8},{8,4},{12,0},{1,13},{5,9},{9,5},{13,1},{2,14},{6,10},... | collective-permute-start | bytes 98312 | tf_op jit(solution)/shard_map/ppermute | solution.py:222
  6.0 0.0 collective-permute-start.1
  6.0 0.6 %collective-permute-start = (bf16[8,2048]{1,0:T(8,128)(2,1)S(1)}, bf16[8,2048]{1,0:T(8,128)(2,1)S(1)}, u32[]{:S(2)}, u32[]{:S(2)}) collective-permute-start(bf16[8,2048]{1,0:T(8,128)(2,1)S(1)} %shard_map.64.refs_0_), channel_id=1, source_target_pairs={{0,4},{4,0},{8,12},{12,8},{1,5},{5,1},{9,13},{13,9},{2,6},{6,2},{1... | collective-permute-start | bytes 98312 | tf_op jit(solution)/shard_map/ppermute | solution.py:222
  6.6 1.3 %collective-permute-done.2.refs_3_ = bf16[8,2048]{1,0:T(8,128)(2,1)S(1)} collective-permute-done((bf16[8,2048]{1,0:T(8,128)(2,1)S(1)}, bf16[8,2048]{1,0:T(8,128)(2,1)S(1)}, u32[]{:S(2)}, u32[]{:S(2)}) %collective-permute-start.2) | collective-permute-done | bytes 32800 | tf_op jit(solution)/shard_map/ppermute | solution.py:222
  7.9 2.9 %collective-permute-done.1.refs_2_ = bf16[8,2048]{1,0:T(8,128)(2,1)S(1)} collective-permute-done((bf16[8,2048]{1,0:T(8,128)(2,1)S(1)}, bf16[8,2048]{1,0:T(8,128)(2,1)S(1)}, u32[]{:S(2)}, u32[]{:S(2)}) %collective-permute-start.1) | collective-permute-done | bytes 32800 | tf_op jit(solution)/shard_map/ppermute | solution.py:222
  10.8 0.0 collective-permute-done.refs_1_
  10.8 0.0 copy-done
  10.8 0.0 copy-done.2
  10.8 3.5 %shard_map.65 = (f32[72,768]{1,0:T(8,128)S(1)}, f32[72,768]{1,0:T(8,128)S(1)}, bf16[32,2048]{1,0:T(8,128)(2,1)S(1)}, f32[8,512]{1,0:T(8,128)S(1)}) custom-call(bf16[8,2048]{1,0:T(8,128)(2,1)S(1)} %shard_map.64.refs_0_, bf16[8,2048]{1,0:T(8,128)(2,1)S(1)} %collective-permute-done.refs_1_, bf16[8,2048]{1,0:T(8,128)(2,1)S(1)} %collective-permute-done.1.refs_2_, ...), custom_call_target="tpu_custom_call" | custom-call | tf_op jit(solution)/shard_map/pallas_call | solution.py:247
  14.3 0.1 collective-permute-start.3
  14.4 0.0 copy-start.3
  14.4 0.0 copy-start.1
  14.4 1.3 %shard_map.66._.begun = f32[128,256]{1,0:T(8,128)S(1)} custom-call(bf16[32,2048]{1,0:T(8,128)(2,1)S(1)} %get-tuple-element.13.scaled, bf16[3,2048,2048]{2,1,0:T(8,128)(2,1)S(1)} %copy-done), custom_call_target="tpu_custom_call" | custom-call | tf_op jit(solution)/shard_map/pallas_call | solution.py:255
  15.8 0.1 collective-permute-done.3.got
  15.9 0.1 shard_map.67._
  16.0 2.4 %shard_map.68 = (f32[72,768]{1,0:T(8,128)S(1)}, f32[72,768]{1,0:T(8,128)S(1)}) custom-call(bf16[32,2048]{1,0:T(8,128)(2,1)S(1)} %get-tuple-element.13.scaled, bf16[3,2048,2048]{2,1,0:T(8,128)(2,1)S(1)} %copy-done, f32[8,512]{1,0:T(8,128)S(1)} %get-tuple-element.14.packed, f32[128,256]{1,0:T(8,128)S(1)} %shard_map.66._.begun, bf16[72,768]{1,0:T(8,128)(2,1)S(1)} %shard_map.67._), custom_call_target="tpu_custom_call" | custom-call | tf_op jit(solution)/shard_map/pallas_call | solution.py:260
  18.4 0.4 %collective-permute-start.4 = (f32[72,768]{1,0:T(8,128)S(1)}, f32[72,768]{1,0:T(8,128)S(1)}, u32[]{:S(2)}, u32[]{:S(2)}) collective-permute-start(f32[72,768]{1,0:T(8,128)S(1)} %get-tuple-element.18), channel_id=1, source_target_pairs={{0,1},{1,0},{2,3},{3,2},{4,5},{5,4},{6,7},{7,6},{8,9},{9,8},{10,11... | collective-permute-start | bytes 663560 | tf_op jit(solution)/shard_map/ppermute | solution.py:222
  18.9 1.5 %collective-permute-start.5 = (bf16[72,768]{1,0:T(8,128)(2,1)S(1)}, bf16[72,768]{1,0:T(8,128)(2,1)S(1)}, u32[]{:S(2)}, u32[]{:S(2)}) collective-permute-start(bf16[72,768]{1,0:T(8,128)(2,1)S(1)} %shard_map.67._), channel_id=1, source_target_pairs={{0,2},{1,3},{2,0},{3,1},{4,6},{5,7},{6,4},{7,5},{8,10},{9,11},{10,... | collective-permute-start | bytes 331784 | tf_op jit(solution)/shard_map/ppermute | solution.py:222
  20.4 0.0 copy-done.3
  20.4 0.2 shard_map.69.long_ref
  20.5 3.4 %collective-permute-done.5.far = bf16[72,768]{1,0:T(8,128)(2,1)S(1)} collective-permute-done((bf16[72,768]{1,0:T(8,128)(2,1)S(1)}, bf16[72,768]{1,0:T(8,128)(2,1)S(1)}, u32[]{:S(2)}, u32[]{:S(2)}) %collective-permute-start.5) | collective-permute-done | bytes 110624 | tf_op jit(solution)/shard_map/ppermute | solution.py:222
  24.0 0.0 collective-permute-done.4.near
  24.0 0.0 copy-done.1
  24.0 0.3 shard_map.70.refs_0_
  24.3 2.5 %collective-permute-start.8 = (bf16[32,512]{1,0:T(8,128)(2,1)S(1)}, bf16[32,512]{1,0:T(8,128)(2,1)S(1)}, u32[]{:S(2)}, u32[]{:S(2)}) collective-permute-start(bf16[32,512]{1,0:T(8,128)(2,1)S(1)} %shard_map.70.refs_0_), channel_id=1, source_target_pairs={{0,12},{4,8},{8,4},{12,0},{1,13},{5,9},{9,5},{13,1},{2,14},{6,10},... | collective-permute-start | bytes 98312 | tf_op jit(solution)/shard_map/ppermute | solution.py:222
  26.8 0.0 collective-permute-start.7
  26.8 2.0 %collective-permute-start.6 = (bf16[32,512]{1,0:T(8,128)(2,1)S(1)}, bf16[32,512]{1,0:T(8,128)(2,1)S(1)}, u32[]{:S(2)}, u32[]{:S(2)}) collective-permute-start(bf16[32,512]{1,0:T(8,128)(2,1)S(1)} %shard_map.70.refs_0_), channel_id=1, source_target_pairs={{0,4},{4,0},{8,12},{12,8},{1,5},{5,1},{9,13},{13,9},{2,6},{6,2},{1... | collective-permute-start | bytes 98312 | tf_op jit(solution)/shard_map/ppermute | solution.py:222
  28.7 1.6 %shard_map.71.refs_4_ = bf16[1,2048,512]{2,1,0:T(8,128)(2,1)S(1)} custom-call(bf16[2048,8192]{1,0:T(8,128)(2,1)} %w_out.3), custom_call_target="tpu_custom_call" | custom-call | tf_op jit(solution)/shard_map/pallas_call | solution.py:264
  30.3 2.9 %shard_map.72.refs_5_ = bf16[3,2048,512]{2,1,0:T(8,128)(2,1)S(1)} custom-call(bf16[2048,8192]{1,0:T(8,128)(2,1)} %w_out.3), custom_call_target="tpu_custom_call" | custom-call | tf_op jit(solution)/shard_map/pallas_call | solution.py:264
  33.3 0.0 collective-permute-done.8.refs_3_
  33.3 0.0 collective-permute-done.7.refs_2_
  33.3 0.0 collective-permute-done.6.refs_1_
  33.3 2.4 %shard_map.73 = (bf16[2,8,2048]{2,1,0:T(8,128)(2,1)S(1)}, f32[2,8,2048]{2,1,0:T(8,128)S(1)}) custom-call(bf16[32,512]{1,0:T(8,128)(2,1)S(1)} %shard_map.70.refs_0_, bf16[32,512]{1,0:T(8,128)(2,1)S(1)} %collective-permute-done.6.refs_1_, bf16[32,512]{1,0:T(8,128)(2,1)S(1)} %collective-permute-done.7.refs_2_, ...), custom_call_target="tpu_custom_call" | custom-call | tf_op jit(solution)/shard_map/pallas_call | solution.py:276
  35.7 0.1 collective-permute-start.9
  35.8 1.2 %collective-permute-done.9.got.near = bf16[2,8,2048]{2,1,0:T(8,128)(2,1)S(1)} collective-permute-done((bf16[2,8,2048]{2,1,0:T(8,128)(2,1)S(1)}, bf16[2,8,2048]{2,1,0:T(8,128)(2,1)S(1)}, u32[]{:S(2)}, u32[]{:S(2)}) %collective-permute-start.9) | collective-permute-done | bytes 65568 | tf_op jit(solution)/shard_map/ppermute | solution.py:222
  37.1 1.6 %collective-permute-start.10 = (bf16[8,2048]{1,0:T(8,128)(2,1)S(1)}, bf16[8,2048]{1,0:T(8,128)(2,1)S(1)}, u32[]{:S(2)}, u32[]{:S(2)}) collective-permute-start(bf16[8,2048]{1,0:T(8,128)(2,1)S(1)} %shard_map.74), channel_id=1, source_target_pairs={{0,2},{1,3},{2,0},{3,1},{4,6},{5,7},{6,4},{7,5},{8,10},{9,11},{10,... | collective-permute-start | bytes 98312 | tf_op jit(solution)/shard_map/ppermute | solution.py:222
  38.6 2.4 %collective-permute-done.10.far = bf16[8,2048]{1,0:T(8,128)(2,1)S(1)} collective-permute-done((bf16[8,2048]{1,0:T(8,128)(2,1)S(1)}, bf16[8,2048]{1,0:T(8,128)(2,1)S(1)}, u32[]{:S(2)}, u32[]{:S(2)}) %collective-permute-start.10) | collective-permute-done | bytes 32800 | tf_op jit(solution)/shard_map/ppermute | solution.py:222
  41.1 0.6 %shard_map.75 = bf16[8,2048]{1,0:T(8,128)(2,1)} custom-call(f32[2,8,2048]{2,1,0:T(8,128)S(1)} %get-tuple-element.19.keep, bf16[2,8,2048]{2,1,0:T(8,128)(2,1)S(1)} %collective-permute-done.9.got.near, bf16[8,2048]{1,0:T(8,128)(2,1)S(1)} %collective-permute-done.10.far), custom_call_target="tpu_custom_call" | custom-call | tf_op jit(solution)/shard_map/pallas_call | solution.py:286
  (2 shorter events, 0.0 us)
Async XLA Ops:
  0.0 10.8 %copy-start = (bf16[3,2048,2048]{2,1,0:T(8,128)(2,1)S(1)}, bf16[3,2048,2048]{2,1,0:T(8,128)(2,1)}, u32[]{:S(2)}) copy-start(bf16[3,2048,2048]{2,1,0:T(8,128)(2,1)} %w_in.3) | copy-start | bytes 75497472
  0.0 10.8 %copy-start.2 = (f32[2048]{0:T(1024)S(1)}, f32[2048]{0:T(1024)}, u32[]{:S(2)}) copy-start(f32[2048]{0:T(1024)} %param.7) | copy-start | bytes 24580
  0.0 0.9 %copy-start.4 = (bf16[8,2048]{1,0:T(8,128)(2,1)S(1)}, bf16[8,2048]{1,0:T(8,128)(2,1)}, u32[]{:S(2)}) copy-start(bf16[8,2048]{1,0:T(8,128)(2,1)} %x_ref.1) | copy-start | bytes 98308
  0.9 7.0 %collective-permute-start.2 = (bf16[8,2048]{1,0:T(8,128)(2,1)S(1)}, bf16[8,2048]{1,0:T(8,128)(2,1)S(1)}, u32[]{:S(2)}, u32[]{:S(2)}) collective-permute-start(bf16[8,2048]{1,0:T(8,128)(2,1)S(1)} %shard_map.64.refs_0_), channel_id=1, source_target_pairs={{0,12},{4,8},{8,4},{12,0},{1,13},{5,9},{9,5},{13,1},{2,14},{6,10},... | collective-permute-start | bytes 98312 | tf_op jit(solution)/shard_map/ppermute | solution.py:222
  6.0 4.8 %collective-permute-start.1 = (bf16[8,2048]{1,0:T(8,128)(2,1)S(1)}, bf16[8,2048]{1,0:T(8,128)(2,1)S(1)}, u32[]{:S(2)}, u32[]{:S(2)}) collective-permute-start(bf16[8,2048]{1,0:T(8,128)(2,1)S(1)} %shard_map.64.refs_0_), channel_id=1, source_target_pairs={{0,8},{4,12},{8,0},{12,4},{1,9},{5,13},{9,1},{13,5},{2,10},{6,14},... | collective-permute-start | bytes 98312 | tf_op jit(solution)/shard_map/ppermute | solution.py:222
  6.0 4.8 %collective-permute-start = (bf16[8,2048]{1,0:T(8,128)(2,1)S(1)}, bf16[8,2048]{1,0:T(8,128)(2,1)S(1)}, u32[]{:S(2)}, u32[]{:S(2)}) collective-permute-start(bf16[8,2048]{1,0:T(8,128)(2,1)S(1)} %shard_map.64.refs_0_), channel_id=1, source_target_pairs={{0,4},{4,0},{8,12},{12,8},{1,5},{5,1},{9,13},{13,9},{2,6},{6,2},{1... | collective-permute-start | bytes 98312 | tf_op jit(solution)/shard_map/ppermute | solution.py:222
  14.3 1.5 %collective-permute-start.3 = (f32[72,768]{1,0:T(8,128)S(1)}, f32[72,768]{1,0:T(8,128)S(1)}, u32[]{:S(2)}, u32[]{:S(2)}) collective-permute-start(f32[72,768]{1,0:T(8,128)S(1)} %get-tuple-element.16), channel_id=1, source_target_pairs={{0,1},{1,0},{2,3},{3,2},{4,5},{5,4},{6,7},{7,6},{8,9},{9,8},{10,11... | collective-permute-start | bytes 663560 | tf_op jit(solution)/shard_map/ppermute | solution.py:222
  14.4 5.9 %copy-start.3 = (f32[7,128]{1,0:T(8,128)S(1)}, f32[7,128]{1,0:T(8,128)}, u32[]{:S(2)}) copy-start(f32[7,128]{1,0:T(8,128)} %se.1) | copy-start | bytes 10756
  14.4 9.6 %copy-start.1 = (f32[3,3,2048]{2,1,0:T(4,128)S(1)}, f32[3,3,2048]{2,1,0:T(4,128)}, u32[]{:S(2)}) copy-start(f32[3,3,2048]{2,1,0:T(4,128)} %short.1) | copy-start | bytes 221188
  18.4 5.5 %collective-permute-start.4 = (f32[72,768]{1,0:T(8,128)S(1)}, f32[72,768]{1,0:T(8,128)S(1)}, u32[]{:S(2)}, u32[]{:S(2)}) collective-permute-start(f32[72,768]{1,0:T(8,128)S(1)} %get-tuple-element.18), channel_id=1, source_target_pairs={{0,1},{1,0},{2,3},{3,2},{4,5},{5,4},{6,7},{7,6},{8,9},{9,8},{10,11... | collective-permute-start | bytes 663560 | tf_op jit(solution)/shard_map/ppermute | solution.py:222
  18.9 5.1 %collective-permute-start.5 = (bf16[72,768]{1,0:T(8,128)(2,1)S(1)}, bf16[72,768]{1,0:T(8,128)(2,1)S(1)}, u32[]{:S(2)}, u32[]{:S(2)}) collective-permute-start(bf16[72,768]{1,0:T(8,128)(2,1)S(1)} %shard_map.67._), channel_id=1, source_target_pairs={{0,2},{1,3},{2,0},{3,1},{4,6},{5,7},{6,4},{7,5},{8,10},{9,11},{10,... | collective-permute-start | bytes 331784 | tf_op jit(solution)/shard_map/ppermute | solution.py:222
  24.3 9.0 %collective-permute-start.8 = (bf16[32,512]{1,0:T(8,128)(2,1)S(1)}, bf16[32,512]{1,0:T(8,128)(2,1)S(1)}, u32[]{:S(2)}, u32[]{:S(2)}) collective-permute-start(bf16[32,512]{1,0:T(8,128)(2,1)S(1)} %shard_map.70.refs_0_), channel_id=1, source_target_pairs={{0,12},{4,8},{8,4},{12,0},{1,13},{5,9},{9,5},{13,1},{2,14},{6,10},... | collective-permute-start | bytes 98312 | tf_op jit(solution)/shard_map/ppermute | solution.py:222
  26.8 6.5 %collective-permute-start.7 = (bf16[32,512]{1,0:T(8,128)(2,1)S(1)}, bf16[32,512]{1,0:T(8,128)(2,1)S(1)}, u32[]{:S(2)}, u32[]{:S(2)}) collective-permute-start(bf16[32,512]{1,0:T(8,128)(2,1)S(1)} %shard_map.70.refs_0_), channel_id=1, source_target_pairs={{0,8},{4,12},{8,0},{12,4},{1,9},{5,13},{9,1},{13,5},{2,10},{6,14},... | collective-permute-start | bytes 98312 | tf_op jit(solution)/shard_map/ppermute | solution.py:222
  26.8 6.5 %collective-permute-start.6 = (bf16[32,512]{1,0:T(8,128)(2,1)S(1)}, bf16[32,512]{1,0:T(8,128)(2,1)S(1)}, u32[]{:S(2)}, u32[]{:S(2)}) collective-permute-start(bf16[32,512]{1,0:T(8,128)(2,1)S(1)} %shard_map.70.refs_0_), channel_id=1, source_target_pairs={{0,4},{4,0},{8,12},{12,8},{1,5},{5,1},{9,13},{13,9},{2,6},{6,2},{1... | collective-permute-start | bytes 98312 | tf_op jit(solution)/shard_map/ppermute | solution.py:222
  35.7 1.3 %collective-permute-start.9 = (bf16[2,8,2048]{2,1,0:T(8,128)(2,1)S(1)}, bf16[2,8,2048]{2,1,0:T(8,128)(2,1)S(1)}, u32[]{:S(2)}, u32[]{:S(2)}) collective-permute-start(bf16[2,8,2048]{2,1,0:T(8,128)(2,1)S(1)} %get-tuple-element.20), channel_id=1, source_target_pairs={{0,1},{1,0},{2,3},{3,2},{4,5},{5,4},{6,7},{7,6},{8,9},{9,8},{10,11... | collective-permute-start | bytes 196616 | tf_op jit(solution)/shard_map/ppermute | solution.py:222
  37.1 4.0 %collective-permute-start.10 = (bf16[8,2048]{1,0:T(8,128)(2,1)S(1)}, bf16[8,2048]{1,0:T(8,128)(2,1)S(1)}, u32[]{:S(2)}, u32[]{:S(2)}) collective-permute-start(bf16[8,2048]{1,0:T(8,128)(2,1)S(1)} %shard_map.74), channel_id=1, source_target_pairs={{0,2},{1,3},{2,0},{3,1},{4,6},{5,7},{6,4},{7,5},{8,10},{9,11},{10,... | collective-permute-start | bytes 98312 | tf_op jit(solution)/shard_map/ppermute | solution.py:222

commit v4 on v3

--- a/solution.py
+++ b/solution.py
@@ -77,6 +77,12 @@
     )
 
 
+def doubled(scaled):
+    count = scaled.shape[0] // 2
+    high, low = spread(scaled[:count]), spread(scaled[count:])
+    return [jnp.concatenate(pair, axis=0) for pair in zip(high, low)]
+
+
 def products(w_in, packs, chip, comp):
     c = lax.axis_index("chan")
     half = w_in.shape[1] // (2 * lax.axis_size("chan"))
@@ -87,7 +93,9 @@
             start = pl.multiple_of((2 * owner + h) * half, half)
             term = contract_last(w_in[comp, pl.ds(start, half), :], packs[2 * other + h])
             total = term if total is None else total + term
-    return total.T
+    flipped = total.T
+    count = flipped.shape[0] // 2
+    return flipped[:count] + flipped[count:]
 
 
 def put(flipped, comp, keep, send):
@@ -113,20 +121,23 @@
         wide[pl.ds(place, rows), :] = pieces[hop][...].astype(F32)
     tokens = wide[...]
     packed[...] = high_low(jnp.sum(tokens * tokens, axis=1, keepdims=True))
-    scaled[...] = (tokens * gain[...]).astype(BF16)
-    packs = spread(scaled[...])
+    exact = tokens * gain[...]
+    high = exact.astype(BF16)
+    scaled[: tokens.shape[0]] = high
+    scaled[tokens.shape[0] :] = (exact - high.astype(F32)).astype(BF16)
+    packs = doubled(scaled[...])
     for comp in range(3):
         put(products(w_in, packs, 1, comp), comp, keep, send)
     put_squares(packed[...], keep, send)
 
 
 def second_body(scaled, w_in, out):
-    out[...] = products(w_in, spread(scaled[...]), 0, 0)
+    out[...] = products(w_in, doubled(scaled[...]), 0, 0)
 
 
 def third_body(scaled, w_in, packed, begun, _, send, keep):
     put(begun[...], 0, keep, send)
-    packs = spread(scaled[...])
+    packs = doubled(scaled[...])
     for comp in (1, 2):
         put(products(w_in, packs, 0, comp), comp, keep, send)
     put_squares(packed[...], keep, send)
@@ -246,18 +257,18 @@
     payload = (struct((wide_rows, wide_columns), F32),) * 2
     send, keep, scaled, packed = call(
         functools.partial(first_body, seq),
-        (*payload, struct((tokens, columns), BF16), struct((8, tokens // 8 * LANES), F32)),
+        (*payload, struct((2 * tokens, columns), BF16), struct((8, tokens // 8 * LANES), F32)),
         [VMEM] * (seq + 2),
         scratch=[pltpu.VMEM((tokens, columns), F32)],
-        limit=10,
+        limit=14,
     )(*pieces, norm_gain.reshape(1, columns), held_in)
     near = swap(send, "chan", 1)
-    begun = call(second_body, struct((PACK * tokens, quarter // 2), F32), [VMEM] * 2, limit=3)(scaled, held_in)
+    begun = call(second_body, struct((PACK * tokens, quarter // 2), F32), [VMEM] * 2, limit=8)(scaled, held_in)
     relay = call(
         functools.partial(relay_body, 2 * tokens), struct((wide_rows, wide_columns), BF16), [VMEM] * 3
     )(keep, near, begun)
     far = swap(relay, "chan", 2)
-    send, keep = call(third_body, payload, [VMEM] * 5, limit=3)(scaled, held_in, packed, begun, relay)
+    send, keep = call(third_body, payload, [VMEM] * 5, limit=8)(scaled, held_in, packed, begun, relay)
     near = swap(send, "chan", 1)
     outputs, w_parts = w_out.shape[0], []
     for hops in (range(SPLIT), range(SPLIT, seq)):

time: 41.8 us -> 42 us (level)
  transfers between devices with their start and end apart: 11 -> 11, of which waited for: 6 -> 5; matrix products, arithmetic and copies ran while one was open for 0% -> 0% of each run, Pallas kernels for 14% -> 15%
where the time goes in v4:
time: 42 us; the launch traced here: 41.9 us
  Pallas kernels  15.7 us (37%)
  starting transfers between devices  13.8 us (33%)
  waiting for transfers between devices  11.3 us (27%)
  local copies, waits for them, and re-layouts  0.93 us (2%)
    ppermute x11, starting transfers between devices, swap(): lax.ppermute(value, axis, [(i, i ^ bit) for i in range(lax.axis_size(axis...  13.8 us
    ppermute x11, waiting for transfers between devices, swap(): lax.ppermute(value, axis, [(i, i ^ bit) for i in range(lax.axis_size(axis...  11.3 us
    pallas_call x2, Pallas kernels, short_shards(): call(functools.partial(load_body, seq, quarter, hops), pltpu.VMEM((len(ho...  4.53 us
    pallas_call x1, Pallas kernels, short_shards(): call(functools.partial(first_body, seq), (*payload, struct((2 * tokens, c...  3.59 us
    pallas_call x1, Pallas kernels, short_shards(): call(third_body, payload, [VMEM] * 5, limit=8)  2.48 us
    pallas_call x1, Pallas kernels, short_shards(): call(functools.partial(output_body, seq, SPLIT), (struct((2, tokens // ch...  2.45 us
    pallas_call x1, Pallas kernels, short_shards(): call(second_body, struct((PACK * tokens, quarter // 2), F32), [VMEM] * 2,...  1.39 us
    unnamed x10, local copies, waits for them, and re-layouts  0.93 us
  transfers between devices with their start and end apart: 11, of which 5 were waited for; matrix products, arithmetic and copies ran while one was open for 0% of the time, Pallas kernels for 15%

profile of v4, /device:TPU:0, one launch (start us, length us, event | category | flops | bytes accessed | tf_op | source)
XLA Modules:
  0.0 41.9 jit_solution(13606697764715181889)
XLA Ops:
  0.0 0.0 copy-start
  0.0 0.0 copy-start.2
  0.0 0.0 copy-start.4
  0.0 0.9 %copy-done.4 = bf16[8,2048]{1,0:T(8,128)(2,1)S(1)} copy-done((bf16[8,2048]{1,0:T(8,128)(2,1)S(1)}, bf16[8,2048]{1,0:T(8,128)(2,1)}, u32[]{:S(2)}) %copy-start.4) | copy-done | bytes 32792
  0.9 5.1 %collective-permute-start.2 = (bf16[8,2048]{1,0:T(8,128)(2,1)S(1)}, bf16[8,2048]{1,0:T(8,128)(2,1)S(1)}, u32[]{:S(2)}, u32[]{:S(2)}) collective-permute-start(bf16[8,2048]{1,0:T(8,128)(2,1)S(1)} %shard_map.64.refs_0_), channel_id=1, source_target_pairs={{0,12},{4,8},{8,4},{12,0},{1,13},{5,9},{9,5},{13,1},{2,14},{6,10},... | collective-permute-start | bytes 98312 | tf_op jit(solution)/shard_map/ppermute | solution.py:233
  6.0 0.0 collective-permute-start.1
  6.0 0.6 %collective-permute-start = (bf16[8,2048]{1,0:T(8,128)(2,1)S(1)}, bf16[8,2048]{1,0:T(8,128)(2,1)S(1)}, u32[]{:S(2)}, u32[]{:S(2)}) collective-permute-start(bf16[8,2048]{1,0:T(8,128)(2,1)S(1)} %shard_map.64.refs_0_), channel_id=1, source_target_pairs={{0,4},{4,0},{8,12},{12,8},{1,5},{5,1},{9,13},{13,9},{2,6},{6,2},{1... | collective-permute-start | bytes 98312 | tf_op jit(solution)/shard_map/ppermute | solution.py:233
  6.6 1.3 %collective-permute-done.2.refs_3_ = bf16[8,2048]{1,0:T(8,128)(2,1)S(1)} collective-permute-done((bf16[8,2048]{1,0:T(8,128)(2,1)S(1)}, bf16[8,2048]{1,0:T(8,128)(2,1)S(1)}, u32[]{:S(2)}, u32[]{:S(2)}) %collective-permute-start.2) | collective-permute-done | bytes 32800 | tf_op jit(solution)/shard_map/ppermute | solution.py:233
  7.9 2.9 %collective-permute-done.1.refs_2_ = bf16[8,2048]{1,0:T(8,128)(2,1)S(1)} collective-permute-done((bf16[8,2048]{1,0:T(8,128)(2,1)S(1)}, bf16[8,2048]{1,0:T(8,128)(2,1)S(1)}, u32[]{:S(2)}, u32[]{:S(2)}) %collective-permute-start.1) | collective-permute-done | bytes 32800 | tf_op jit(solution)/shard_map/ppermute | solution.py:233
  10.8 0.0 collective-permute-done.refs_1_
  10.8 0.0 copy-done
  10.8 0.0 copy-done.2
  10.8 3.6 %shard_map.65 = (f32[72,768]{1,0:T(8,128)S(1)}, f32[72,768]{1,0:T(8,128)S(1)}, bf16[64,2048]{1,0:T(8,128)(2,1)S(1)}, f32[8,512]{1,0:T(8,128)S(1)}) custom-call(bf16[8,2048]{1,0:T(8,128)(2,1)S(1)} %shard_map.64.refs_0_, bf16[8,2048]{1,0:T(8,128)(2,1)S(1)} %collective-permute-done.refs_1_, bf16[8,2048]{1,0:T(8,128)(2,1)S(1)} %collective-permute-done.1.refs_2_, ...), custom_call_target="tpu_custom_call" | custom-call | tf_op jit(solution)/shard_map/pallas_call | solution.py:258
  14.4 0.1 collective-permute-start.3
  14.5 0.0 copy-start.3
  14.5 0.0 copy-start.1
  14.5 1.4 %shard_map.66._.begun = f32[128,256]{1,0:T(8,128)S(1)} custom-call(bf16[64,2048]{1,0:T(8,128)(2,1)S(1)} %get-tuple-element.13.scaled, bf16[3,2048,2048]{2,1,0:T(8,128)(2,1)S(1)} %copy-done), custom_call_target="tpu_custom_call" | custom-call | tf_op jit(solution)/shard_map/pallas_call | solution.py:266
  15.9 0.0 collective-permute-done.3.got
  16.0 0.1 shard_map.67._
  16.1 2.5 %shard_map.68 = (f32[72,768]{1,0:T(8,128)S(1)}, f32[72,768]{1,0:T(8,128)S(1)}) custom-call(bf16[64,2048]{1,0:T(8,128)(2,1)S(1)} %get-tuple-element.13.scaled, bf16[3,2048,2048]{2,1,0:T(8,128)(2,1)S(1)} %copy-done, f32[8,512]{1,0:T(8,128)S(1)} %get-tuple-element.14.packed, f32[128,256]{1,0:T(8,128)S(1)} %shard_map.66._.begun, bf16[72,768]{1,0:T(8,128)(2,1)S(1)} %shard_map.67._), custom_call_target="tpu_custom_call" | custom-call | tf_op jit(solution)/shard_map/pallas_call | solution.py:271
  18.6 0.5 %collective-permute-start.4 = (f32[72,768]{1,0:T(8,128)S(1)}, f32[72,768]{1,0:T(8,128)S(1)}, u32[]{:S(2)}, u32[]{:S(2)}) collective-permute-start(f32[72,768]{1,0:T(8,128)S(1)} %get-tuple-element.18), channel_id=1, source_target_pairs={{0,1},{1,0},{2,3},{3,2},{4,5},{5,4},{6,7},{7,6},{8,9},{9,8},{10,11... | collective-permute-start | bytes 663560 | tf_op jit(solution)/shard_map/ppermute | solution.py:233
  19.1 1.5 %collective-permute-start.5 = (bf16[72,768]{1,0:T(8,128)(2,1)S(1)}, bf16[72,768]{1,0:T(8,128)(2,1)S(1)}, u32[]{:S(2)}, u32[]{:S(2)}) collective-permute-start(bf16[72,768]{1,0:T(8,128)(2,1)S(1)} %shard_map.67._), channel_id=1, source_target_pairs={{0,2},{1,3},{2,0},{3,1},{4,6},{5,7},{6,4},{7,5},{8,10},{9,11},{10,... | collective-permute-start | bytes 331784 | tf_op jit(solution)/shard_map/ppermute | solution.py:233
  20.6 0.0 copy-done.3
  20.6 0.2 shard_map.69.long_ref
  20.8 3.4 %collective-permute-done.5.far = bf16[72,768]{1,0:T(8,128)(2,1)S(1)} collective-permute-done((bf16[72,768]{1,0:T(8,128)(2,1)S(1)}, bf16[72,768]{1,0:T(8,128)(2,1)S(1)}, u32[]{:S(2)}, u32[]{:S(2)}) %collective-permute-start.5) | collective-permute-done | bytes 110624 | tf_op jit(solution)/shard_map/ppermute | solution.py:233
  24.1 0.0 collective-permute-done.4.near
  24.1 0.0 copy-done.1
  24.1 0.3 shard_map.70.refs_0_
  24.4 2.5 %collective-permute-start.8 = (bf16[32,512]{1,0:T(8,128)(2,1)S(1)}, bf16[32,512]{1,0:T(8,128)(2,1)S(1)}, u32[]{:S(2)}, u32[]{:S(2)}) collective-permute-start(bf16[32,512]{1,0:T(8,128)(2,1)S(1)} %shard_map.70.refs_0_), channel_id=1, source_target_pairs={{0,12},{4,8},{8,4},{12,0},{1,13},{5,9},{9,5},{13,1},{2,14},{6,10},... | collective-permute-start | bytes 98312 | tf_op jit(solution)/shard_map/ppermute | solution.py:233
  26.9 0.0 collective-permute-start.7
  26.9 2.0 %collective-permute-start.6 = (bf16[32,512]{1,0:T(8,128)(2,1)S(1)}, bf16[32,512]{1,0:T(8,128)(2,1)S(1)}, u32[]{:S(2)}, u32[]{:S(2)}) collective-permute-start(bf16[32,512]{1,0:T(8,128)(2,1)S(1)} %shard_map.70.refs_0_), channel_id=1, source_target_pairs={{0,4},{4,0},{8,12},{12,8},{1,5},{5,1},{9,13},{13,9},{2,6},{6,2},{1... | collective-permute-start | bytes 98312 | tf_op jit(solution)/shard_map/ppermute | solution.py:233
  28.9 1.6 %shard_map.71.refs_4_ = bf16[1,2048,512]{2,1,0:T(8,128)(2,1)S(1)} custom-call(bf16[2048,8192]{1,0:T(8,128)(2,1)} %w_out.3), custom_call_target="tpu_custom_call" | custom-call | tf_op jit(solution)/shard_map/pallas_call | solution.py:275
  30.5 2.9 %shard_map.72.refs_5_ = bf16[3,2048,512]{2,1,0:T(8,128)(2,1)S(1)} custom-call(bf16[2048,8192]{1,0:T(8,128)(2,1)} %w_out.3), custom_call_target="tpu_custom_call" | custom-call | tf_op jit(solution)/shard_map/pallas_call | solution.py:275
  33.4 0.0 collective-permute-done.8.refs_3_
  33.4 0.0 collective-permute-done.7.refs_2_
  33.4 0.0 collective-permute-done.6.refs_1_
  33.5 2.5 %shard_map.73 = (bf16[2,8,2048]{2,1,0:T(8,128)(2,1)S(1)}, f32[2,8,2048]{2,1,0:T(8,128)S(1)}) custom-call(bf16[32,512]{1,0:T(8,128)(2,1)S(1)} %shard_map.70.refs_0_, bf16[32,512]{1,0:T(8,128)(2,1)S(1)} %collective-permute-done.6.refs_1_, bf16[32,512]{1,0:T(8,128)(2,1)S(1)} %collective-permute-done.7.refs_2_, ...), custom_call_target="tpu_custom_call" | custom-call | tf_op jit(solution)/shard_map/pallas_call | solution.py:287
  35.9 0.1 collective-permute-start.9
  36.0 1.2 %collective-permute-done.9.got.near = bf16[2,8,2048]{2,1,0:T(8,128)(2,1)S(1)} collective-permute-done((bf16[2,8,2048]{2,1,0:T(8,128)(2,1)S(1)}, bf16[2,8,2048]{2,1,0:T(8,128)(2,1)S(1)}, u32[]{:S(2)}, u32[]{:S(2)}) %collective-permute-start.9) | collective-permute-done | bytes 65568 | tf_op jit(solution)/shard_map/ppermute | solution.py:233
  37.2 1.6 %collective-permute-start.10 = (bf16[8,2048]{1,0:T(8,128)(2,1)S(1)}, bf16[8,2048]{1,0:T(8,128)(2,1)S(1)}, u32[]{:S(2)}, u32[]{:S(2)}) collective-permute-start(bf16[8,2048]{1,0:T(8,128)(2,1)S(1)} %shard_map.74), channel_id=1, source_target_pairs={{0,2},{1,3},{2,0},{3,1},{4,6},{5,7},{6,4},{7,5},{8,10},{9,11},{10,... | collective-permute-start | bytes 98312 | tf_op jit(solution)/shard_map/ppermute | solution.py:233
  38.8 2.4 %collective-permute-done.10.far = bf16[8,2048]{1,0:T(8,128)(2,1)S(1)} collective-permute-done((bf16[8,2048]{1,0:T(8,128)(2,1)S(1)}, bf16[8,2048]{1,0:T(8,128)(2,1)S(1)}, u32[]{:S(2)}, u32[]{:S(2)}) %collective-permute-start.10) | collective-permute-done | bytes 32800 | tf_op jit(solution)/shard_map/ppermute | solution.py:233
  41.2 0.6 %shard_map.75 = bf16[8,2048]{1,0:T(8,128)(2,1)} custom-call(f32[2,8,2048]{2,1,0:T(8,128)S(1)} %get-tuple-element.19.keep, bf16[2,8,2048]{2,1,0:T(8,128)(2,1)S(1)} %collective-permute-done.9.got.near, bf16[8,2048]{1,0:T(8,128)(2,1)S(1)} %collective-permute-done.10.far), custom_call_target="tpu_custom_call" | custom-call | tf_op jit(solution)/shard_map/pallas_call | solution.py:297
  (2 shorter events, 0.0 us)
Async XLA Ops:
  0.0 10.8 %copy-start = (bf16[3,2048,2048]{2,1,0:T(8,128)(2,1)S(1)}, bf16[3,2048,2048]{2,1,0:T(8,128)(2,1)}, u32[]{:S(2)}) copy-start(bf16[3,2048,2048]{2,1,0:T(8,128)(2,1)} %w_in.3) | copy-start | bytes 75497472
  0.0 10.8 %copy-start.2 = (f32[2048]{0:T(1024)S(1)}, f32[2048]{0:T(1024)}, u32[]{:S(2)}) copy-start(f32[2048]{0:T(1024)} %param.7) | copy-start | bytes 24580
  0.0 0.9 %copy-start.4 = (bf16[8,2048]{1,0:T(8,128)(2,1)S(1)}, bf16[8,2048]{1,0:T(8,128)(2,1)}, u32[]{:S(2)}) copy-start(bf16[8,2048]{1,0:T(8,128)(2,1)} %x_ref.1) | copy-start | bytes 98308
  0.9 7.0 %collective-permute-start.2 = (bf16[8,2048]{1,0:T(8,128)(2,1)S(1)}, bf16[8,2048]{1,0:T(8,128)(2,1)S(1)}, u32[]{:S(2)}, u32[]{:S(2)}) collective-permute-start(bf16[8,2048]{1,0:T(8,128)(2,1)S(1)} %shard_map.64.refs_0_), channel_id=1, source_target_pairs={{0,12},{4,8},{8,4},{12,0},{1,13},{5,9},{9,5},{13,1},{2,14},{6,10},... | collective-permute-start | bytes 98312 | tf_op jit(solution)/shard_map/ppermute | solution.py:233
  6.0 4.8 %collective-permute-start.1 = (bf16[8,2048]{1,0:T(8,128)(2,1)S(1)}, bf16[8,2048]{1,0:T(8,128)(2,1)S(1)}, u32[]{:S(2)}, u32[]{:S(2)}) collective-permute-start(bf16[8,2048]{1,0:T(8,128)(2,1)S(1)} %shard_map.64.refs_0_), channel_id=1, source_target_pairs={{0,8},{4,12},{8,0},{12,4},{1,9},{5,13},{9,1},{13,5},{2,10},{6,14},... | collective-permute-start | bytes 98312 | tf_op jit(solution)/shard_map/ppermute | solution.py:233
  6.0 4.8 %collective-permute-start = (bf16[8,2048]{1,0:T(8,128)(2,1)S(1)}, bf16[8,2048]{1,0:T(8,128)(2,1)S(1)}, u32[]{:S(2)}, u32[]{:S(2)}) collective-permute-start(bf16[8,2048]{1,0:T(8,128)(2,1)S(1)} %shard_map.64.refs_0_), channel_id=1, source_target_pairs={{0,4},{4,0},{8,12},{12,8},{1,5},{5,1},{9,13},{13,9},{2,6},{6,2},{1... | collective-permute-start | bytes 98312 | tf_op jit(solution)/shard_map/ppermute | solution.py:233
  14.4 1.5 %collective-permute-start.3 = (f32[72,768]{1,0:T(8,128)S(1)}, f32[72,768]{1,0:T(8,128)S(1)}, u32[]{:S(2)}, u32[]{:S(2)}) collective-permute-start(f32[72,768]{1,0:T(8,128)S(1)} %get-tuple-element.16), channel_id=1, source_target_pairs={{0,1},{1,0},{2,3},{3,2},{4,5},{5,4},{6,7},{7,6},{8,9},{9,8},{10,11... | collective-permute-start | bytes 663560 | tf_op jit(solution)/shard_map/ppermute | solution.py:233
  14.5 6.1 %copy-start.3 = (f32[7,128]{1,0:T(8,128)S(1)}, f32[7,128]{1,0:T(8,128)}, u32[]{:S(2)}) copy-start(f32[7,128]{1,0:T(8,128)} %se.1) | copy-start | bytes 10756
  14.5 9.6 %copy-start.1 = (f32[3,3,2048]{2,1,0:T(4,128)S(1)}, f32[3,3,2048]{2,1,0:T(4,128)}, u32[]{:S(2)}) copy-start(f32[3,3,2048]{2,1,0:T(4,128)} %short.1) | copy-start | bytes 221188
  18.6 5.5 %collective-permute-start.4 = (f32[72,768]{1,0:T(8,128)S(1)}, f32[72,768]{1,0:T(8,128)S(1)}, u32[]{:S(2)}, u32[]{:S(2)}) collective-permute-start(f32[72,768]{1,0:T(8,128)S(1)} %get-tuple-element.18), channel_id=1, source_target_pairs={{0,1},{1,0},{2,3},{3,2},{4,5},{5,4},{6,7},{7,6},{8,9},{9,8},{10,11... | collective-permute-start | bytes 663560 | tf_op jit(solution)/shard_map/ppermute | solution.py:233
  19.1 5.0 %collective-permute-start.5 = (bf16[72,768]{1,0:T(8,128)(2,1)S(1)}, bf16[72,768]{1,0:T(8,128)(2,1)S(1)}, u32[]{:S(2)}, u32[]{:S(2)}) collective-permute-start(bf16[72,768]{1,0:T(8,128)(2,1)S(1)} %shard_map.67._), channel_id=1, source_target_pairs={{0,2},{1,3},{2,0},{3,1},{4,6},{5,7},{6,4},{7,5},{8,10},{9,11},{10,... | collective-permute-start | bytes 331784 | tf_op jit(solution)/shard_map/ppermute | solution.py:233
  24.4 9.0 %collective-permute-start.8 = (bf16[32,512]{1,0:T(8,128)(2,1)S(1)}, bf16[32,512]{1,0:T(8,128)(2,1)S(1)}, u32[]{:S(2)}, u32[]{:S(2)}) collective-permute-start(bf16[32,512]{1,0:T(8,128)(2,1)S(1)} %shard_map.70.refs_0_), channel_id=1, source_target_pairs={{0,12},{4,8},{8,4},{12,0},{1,13},{5,9},{9,5},{13,1},{2,14},{6,10},... | collective-permute-start | bytes 98312 | tf_op jit(solution)/shard_map/ppermute | solution.py:233
  26.9 6.5 %collective-permute-start.7 = (bf16[32,512]{1,0:T(8,128)(2,1)S(1)}, bf16[32,512]{1,0:T(8,128)(2,1)S(1)}, u32[]{:S(2)}, u32[]{:S(2)}) collective-permute-start(bf16[32,512]{1,0:T(8,128)(2,1)S(1)} %shard_map.70.refs_0_), channel_id=1, source_target_pairs={{0,8},{4,12},{8,0},{12,4},{1,9},{5,13},{9,1},{13,5},{2,10},{6,14},... | collective-permute-start | bytes 98312 | tf_op jit(solution)/shard_map/ppermute | solution.py:233
  26.9 6.5 %collective-permute-start.6 = (bf16[32,512]{1,0:T(8,128)(2,1)S(1)}, bf16[32,512]{1,0:T(8,128)(2,1)S(1)}, u32[]{:S(2)}, u32[]{:S(2)}) collective-permute-start(bf16[32,512]{1,0:T(8,128)(2,1)S(1)} %shard_map.70.refs_0_), channel_id=1, source_target_pairs={{0,4},{4,0},{8,12},{12,8},{1,5},{5,1},{9,13},{13,9},{2,6},{6,2},{1... | collective-permute-start | bytes 98312 | tf_op jit(solution)/shard_map/ppermute | solution.py:233
  35.9 1.3 %collective-permute-start.9 = (bf16[2,8,2048]{2,1,0:T(8,128)(2,1)S(1)}, bf16[2,8,2048]{2,1,0:T(8,128)(2,1)S(1)}, u32[]{:S(2)}, u32[]{:S(2)}) collective-permute-start(bf16[2,8,2048]{2,1,0:T(8,128)(2,1)S(1)} %get-tuple-element.20), channel_id=1, source_target_pairs={{0,1},{1,0},{2,3},{3,2},{4,5},{5,4},{6,7},{7,6},{8,9},{9,8},{10,11... | collective-permute-start | bytes 196616 | tf_op jit(solution)/shard_map/ppermute | solution.py:233
  37.2 4.0 %collective-permute-start.10 = (bf16[8,2048]{1,0:T(8,128)(2,1)S(1)}, bf16[8,2048]{1,0:T(8,128)(2,1)S(1)}, u32[]{:S(2)}, u32[]{:S(2)}) collective-permute-start(bf16[8,2048]{1,0:T(8,128)(2,1)S(1)} %shard_map.74), channel_id=1, source_target_pairs={{0,2},{1,3},{2,0},{3,1},{4,6},{5,7},{6,4},{7,5},{8,10},{9,11},{10,... | collective-permute-start | bytes 98312 | tf_op jit(solution)/shard_map/ppermute | solution.py:233
